TPU v7x, 32 devices: a whole 2x2x4 slice. The times are simulated.
32 devices in a mesh: blk: 8 (over z, y), aux: 4 (over x, core).
Axes of the slice: x: 2, y: 2, z: 4, core: 2. Of those that a mesh axis runs over, the one named last changes fastest.
Arguments:
- adjoint: bfloat16 [1024, 1024], P(('blk', 'aux')), may hold values from -0.1875 to 0.1875
- three_centre: bfloat16 [128, 32, 32, 1024], P(('blk', 'aux')), may hold values from -1 to 1
- occ_density: bfloat16 [64, 1024], P('blk'), may hold values from -1 to 1
- vir_density: bfloat16 [64, 1024], P('blk'), may hold values from -1 to 1
- block_sizes: int32 [64], P('blk'), may hold values from 16 to 32
- tile_rows: int32 [128], P(('blk', 'aux')), may hold values from 0 to 7
- col_owner: int32 [128, 1], P(('blk', 'aux')), may hold values from 0 to 7; in each aligned block of 16 rows (0 to 15, 16 to 31, ...) at most 4 rows name the same one
- col_block: int32 [128], P(('blk', 'aux')), may hold values from 0 to 7
Outputs:
- occ_grad: float32 [64, 1024], P(('blk', 'aux'))
- vir_grad: float32 [64, 1024], P(('blk', 'aux'))
Inputs may be any that keep to these rules, and one draw needn't show every extreme that they name: `col_owner`: among the 16 tiles of one blk index (aligned blocks of 16 tiles), at most 4 name the same owner, and some blk index reaches 4.
All inputs are finite; a program needn't handle non-finite values.
Results may differ from a plain program's by a relative error of at most 0.0041.
Values may be sent and summed in bfloat16 or wider, within the bound.
A program may use at most 128 MiB of HBM per device.

v0:
```python
import functools

import jax
import jax.numpy as jnp
from jax import lax
from jax.experimental import pallas as pl
from jax.experimental.pallas import tpu as pltpu
from jax.sharding import PartitionSpec as P

BS = 32
CHUNK = 256
MESH = pl.DeviceIdType.MESH
F32 = jnp.float32
BF16 = jnp.bfloat16


def iota(shape, dim):
    return lax.broadcasted_iota(jnp.int32, shape, dim)


def fold(minor, pairs):
    index = iota((pairs, 128), 0)
    index = index % BS if minor else index // BS
    return (index == iota((pairs, 128), 1) % BS).astype(BF16)


def dot(left, right):
    return jnp.dot(left, right, preferred_element_type=F32)


def dot_nt(left, right):
    return lax.dot_general(left, right, (((1,), (1,)), ((), ())), preferred_element_type=F32)


def fused_kernel(
    n_blk, n_aux, norm,
    sizes, rows, owners, blocks, adj_ref, occ_ref, vir_ref, t_hbm,
    out_ref,
    got, tbuf, cbuf, occ_rep, vir_rep, occ_sums, vir_sums, occ_send, vir_send, occ_got, vir_got,
    t_sem, send_sem, recv_sem, occ_sems, vir_sems,
):
    n_dev = n_blk * n_aux
    occ_out, vir_out = out_ref.at[0], out_ref.at[1]
    depth = n_blk // 2
    count, pairs, naux = tbuf.shape
    own = occ_out.shape[0]
    arows = adj_ref.shape[0]
    span = naux // depth
    per_plane = n_dev // depth
    b = lax.axis_index("blk")
    a = lax.axis_index("aux")
    z, y, x, c = b // 2, b % 2, a // 2, a % 2
    up, down, over_x, over_y, mate = range(5)
    place = {
        up: (b + 2, a),
        down: (b - 2, a),
        over_x: (b, (1 - x) * 2 + c),
        over_y: (z * 2 + 1 - y, a),
        mate: (b, x * 2 + 1 - c),
    }
    has_up, has_down = z < depth - 1, z > 0
    me = b * n_aux + a

    def ident(xx, yy, zz, cc):
        return ((zz * 2 + yy) * 2 + xx) * 2 + cc

    barrier = pltpu.get_barrier_semaphore()

    def greet(k, carry):
        p = lax.rem(me + k, n_dev)
        pl.semaphore_signal(barrier, inc=1, device_id=(p // n_aux, p % n_aux), device_id_type=MESH)
        return carry

    lax.fori_loop(1, n_dev, greet, 0)
    fetches = [pltpu.make_async_copy(t_hbm.at[t], tbuf.at[t], t_sem.at[t]) for t in range(count)]
    for fetch in fetches:
        fetch.start()

    lane = iota((1, pairs), 1)
    major, minor = lane // BS, lane % BS
    got[me, :arows, :] = adj_ref[...]
    vir_all = vir_ref[...].astype(F32)
    slot = iota(vir_all.shape, 0)
    mine = []
    for r in range(own):
        size = sizes[a * own + r]
        row = jnp.sum(jnp.where(slot == a * own + r, vir_all, 0.0), axis=0, keepdims=True)
        mine.append(jnp.where((major < size) & (minor < size), row, 0.0))
    got[me, arows:, :] = jnp.concatenate(mine, axis=0).astype(BF16)

    diag = iota((BS, pairs), 1) // BS == iota((BS, pairs), 0)
    fold_minor = fold(True, pairs)
    pl.semaphore_wait(barrier, n_dev - 1)

    def copy(way, block):
        return pltpu.make_async_remote_copy(
            src_ref=got.at[block],
            dst_ref=got.at[block],
            send_sem=send_sem.at[way, block],
            recv_sem=recv_sem.at[block],
            device_id=place[way],
            device_id_type=MESH,
        )

    def send(way, block, when=None):
        if when is None:
            copy(way, block).start()
        else:

            @pl.when(when)
            def _():
                copy(way, block).start()

    def arrive(block):
        copy(mate, block).wait_recv()

    send(up, me, has_up)
    send(down, me, has_down)
    send(over_x, me)
    send(over_y, me)
    send(mate, me)

    occ_all = occ_ref[...].astype(F32)
    parts = []
    for t in range(count):
        size = sizes[rows[t]]
        row = jnp.sum(jnp.where(slot == rows[t], occ_all, 0.0), axis=0, keepdims=True)
        row = jnp.where((major < size) & (minor < size), row, 0.0)
        parts.append(jnp.where(diag, row, 0.0))
    spread = (iota((128, pairs), 0) == iota((128, pairs), 1) // BS).astype(BF16)
    square = dot(jnp.concatenate(parts, axis=0).astype(BF16), fold_minor)
    occ_rep[...] = dot(square.astype(BF16), spread).reshape(occ_rep.shape)

    def column(zz, from_up):
        block = ident(x, y, zz, c)
        arrive(block)
        if from_up:
            send(down, block, has_down)
        else:
            send(up, block, has_up)
        send(over_x, block)
        send(over_y, block)
        send(mate, block)

    def sides(zz, _):
        block = ident(1 - x, y, zz, c)
        arrive(block)
        send(over_y, block, zz % 2 == 0)
        send(mate, block)
        block = ident(x, 1 - y, zz, c)
        arrive(block)
        send(over_x, block, zz % 2 == 1)
        send(mate, block)

    def corner(zz, _):
        block = ident(1 - x, 1 - y, zz, c)
        arrive(block)
        send(mate, block)

    def mates(zz, _):
        for xx in (x, 1 - x):
            for yy in (y, 1 - y):
                arrive(ident(xx, yy, zz, 1 - c))

    def contract(zz, first, last):
        part = got[pl.ds(zz * per_plane, per_plane), :arows, :].reshape(span, naux)
        columns = pl.ds(pl.multiple_of(zz * span, span), span)

        def step(t, carry):
            cbuf[t, :, columns] = dot_nt(tbuf[t], part).astype(BF16)
            return carry

        lax.fori_loop(first, last, step, 0)

    def planes(dist, work):
        if dist == 0:
            work(z, None)
        elif dist < depth:

            @pl.when(z + dist < depth)
            def _():
                work(z + dist, True)

            @pl.when(z - dist >= 0)
            def _():
                work(z - dist, False)

    def whole(zz, _):
        mates(zz, _)
        contract(zz, 0, count)

    planes(1, column)
    planes(0, sides)
    planes(2, column)
    planes(1, sides)
    planes(0, corner)
    for fetch in fetches:
        fetch.wait()
    mates(z, None)
    contract(z, 0, count // 2)
    planes(3, column)
    contract(z, count // 2, count)
    for dist in range(1, depth):
        planes(dist, corner)
        planes(dist + 1, sides)
        planes(dist, whole)
        planes(dist + 3, column)

    parts = []
    for t in range(count):
        home = owners[t] * n_aux + blocks[t] // own
        near = got[home, arows:, :].astype(F32)
        row = jnp.sum(jnp.where(iota(near.shape, 0) == blocks[t] % own, near, 0.0), axis=0, keepdims=True)
        parts.append(jnp.where(diag, row, 0.0))
    square = dot(jnp.concatenate(parts, axis=0).astype(BF16), fold_minor)
    vir_rep[...] = jnp.concatenate([square] * (pairs // 128), axis=1).reshape(vir_rep.shape)

    def tile(t, carry):
        acc = jnp.zeros((BS, pairs), F32)
        lines = []
        for first in range(0, pairs, CHUNK):
            gram = dot_nt(cbuf[t, first : first + CHUNK, :], tbuf[t])
            for at in range(CHUNK // BS):
                i = first // BS + at
                block_i = gram[at * BS : (at + 1) * BS, :]
                acc = acc + block_i * occ_rep[t, i : i + 1, :]
                lines.append(jnp.sum(block_i * vir_rep[t], axis=0, keepdims=True))
        vir_sums[t] = acc
        occ_sums[t] = jnp.concatenate(lines, axis=0)
        return carry

    lax.fori_loop(0, count, tile, 0)

    def flatten(mat, folding):
        high = mat.astype(BF16)
        low = (mat - high.astype(F32)).astype(BF16)
        both = dot(high, folding) + dot(low, folding)
        lines = []
        for t in range(count):
            wide = jnp.concatenate([both[t * BS : (t + 1) * BS]] * (pairs // 128), axis=1)
            lines.append(jnp.sum(jnp.where(diag, wide, 0.0), axis=0, keepdims=True))
        return lines

    vir_flat = flatten(vir_sums[...].reshape(count * BS, pairs), fold_minor)
    shape = (n_dev, own, 1)
    place_id = iota(shape, 0) * own + iota(shape, 1)
    total = jnp.zeros(vir_send.shape, F32)
    for t in range(count):
        hot = (place_id == owners[t] * (n_aux * own) + blocks[t]).astype(F32)
        total = total + hot * vir_flat[t].reshape(1, 1, pairs)
    vir_send[...] = total.astype(BF16)
    occ_flat = flatten(occ_sums[...].reshape(count * BS, pairs), fold(False, pairs))
    shape = (n_aux, own, 1)
    place_id = iota(shape, 0) * own + iota(shape, 1)
    total = jnp.zeros(occ_send.shape, F32)
    for t in range(count):
        hot = (place_id == rows[t]).astype(F32)
        total = total + hot * occ_flat[t].reshape(1, 1, pairs)
    occ_send[...] = total

    trade(
        n_blk, n_aux, norm, sizes, occ_send, vir_send, occ_out, vir_out, occ_got, vir_got, occ_sems, vir_sems
    )

    for zz in range(depth):
        block = ident(x, y, zz, c)
        for way in (over_x, over_y, mate):
            copy(way, block).wait_send()

        @pl.when((zz <= z) & has_up)
        def _():
            copy(up, ident(x, y, zz, c)).wait_send()

        @pl.when((zz >= z) & has_down)
        def _():
            copy(down, ident(x, y, zz, c)).wait_send()

        block = ident(1 - x, y, zz, c)
        copy(mate, block).wait_send()
        if zz % 2 == 0:
            copy(over_y, block).wait_send()
        block = ident(x, 1 - y, zz, c)
        copy(mate, block).wait_send()
        if zz % 2 == 1:
            copy(over_x, block).wait_send()
        copy(mate, ident(1 - x, 1 - y, zz, c)).wait_send()


def fused(sizes, rows, owners, blocks, adj, occ, vir, three, n_blk, n_aux, norm):
    n_dev = n_blk * n_aux
    count, pairs, naux = three.shape
    own = occ.shape[0] // n_aux
    smem = pl.BlockSpec(memory_space=pltpu.SMEM)
    vmem = pl.BlockSpec(memory_space=pltpu.VMEM)
    square = pltpu.VMEM((count, BS, pairs), F32)
    return pl.pallas_call(
        functools.partial(fused_kernel, n_blk, n_aux, norm),
        out_shape=jax.ShapeDtypeStruct((2, own, pairs), F32),
        in_specs=[smem] * 4 + [vmem] * 3 + [pl.BlockSpec(memory_space=pl.ANY)],
        out_specs=vmem,
        scratch_shapes=[
            pltpu.VMEM((n_dev, adj.shape[0] + own, naux), BF16),
            pltpu.VMEM((count, pairs, naux), BF16),
            pltpu.VMEM((count, pairs, naux), BF16),
            square,
            square,
            square,
            square,
            pltpu.VMEM((n_aux, own, pairs), F32),
            pltpu.VMEM((n_dev, own, pairs), BF16),
            pltpu.VMEM((n_aux, own, pairs), F32),
            pltpu.VMEM((n_dev, own, pairs), BF16),
            pltpu.SemaphoreType.DMA((count,)),
            pltpu.SemaphoreType.DMA((5, n_dev)),
            pltpu.SemaphoreType.DMA((n_dev,)),
            pltpu.SemaphoreType.DMA((2, n_aux)),
            pltpu.SemaphoreType.DMA((2, n_dev)),
        ],
        compiler_params=pltpu.CompilerParams(
            collective_id=0, has_side_effects=True, vmem_limit_bytes=67043328
        ),
        name="fused",
    )(sizes, rows, owners, blocks, adj, occ, vir, three)


def tile_kernel(
    n_aux, own, sizes, rows, owners, blocks, occ_ref, vir_ref, adj_ref, t_ref, occ_out, vir_out, vir_acc
):
    t = pl.program_id(0)
    pairs = BS * BS
    naux = adj_ref.shape[0]

    @pl.when(t == 0)
    def _():
        occ_out[...] = jnp.zeros_like(occ_out)
        vir_acc[...] = jnp.zeros_like(vir_acc)

    row, owner, block = rows[t], owners[t], blocks[t]
    size = sizes[row]
    lane = iota((1, pairs), 1)
    inside = (lane // BS < size) & (lane % BS < size)
    occ_all = occ_ref[...].astype(F32)
    occ_row = jnp.sum(jnp.where(iota(occ_all.shape, 0) == row, occ_all, 0.0), axis=0, keepdims=True)
    occ_row = jnp.where(inside, occ_row, 0.0)
    home = owner * n_aux + block // own
    vir_all = vir_ref[home].astype(F32)
    vir_row = jnp.sum(jnp.where(iota(vir_all.shape, 0) == block % own, vir_all, 0.0), axis=0, keepdims=True)
    diag = iota((BS, pairs), 1) // BS == iota((BS, pairs), 0)
    fold_minor = (iota((pairs, 128), 0) % BS == iota((pairs, 128), 1) % BS).astype(BF16)
    fold_major = (iota((pairs, 128), 0) // BS == iota((pairs, 128), 1) % BS).astype(BF16)
    spread = (iota((128, pairs), 0) == iota((128, pairs), 1) // BS).astype(BF16)
    repeat = pairs // 128

    def square(flat):
        return jnp.dot(jnp.where(diag, flat, 0.0).astype(BF16), fold_minor, preferred_element_type=F32)

    occ_rep = jnp.dot(square(occ_row).astype(BF16), spread, preferred_element_type=F32)
    vir_rep = jnp.concatenate([square(vir_row)] * repeat, axis=1)

    nt = (((1,), (1,)), ((), ()))
    acc = jnp.zeros((BS, pairs), F32)
    lines = []
    for first in range(0, pairs, CHUNK):
        part = lax.dot_general(t_ref[0, first : first + CHUNK, :], adj_ref[...], nt, preferred_element_type=F32)
        gram = lax.dot_general(part.astype(BF16), t_ref[0], nt, preferred_element_type=F32)
        for at in range(CHUNK // BS):
            i = first // BS + at
            block_i = gram[at * BS : (at + 1) * BS, :]
            acc = acc + block_i * occ_rep[i : i + 1, :]
            lines.append(jnp.sum(block_i * vir_rep, axis=0, keepdims=True))
    zmat = jnp.concatenate(lines, axis=0)

    def flatten(mat, fold):
        high = mat.astype(BF16)
        low = (mat - high.astype(F32)).astype(BF16)
        both = jnp.dot(high, fold, preferred_element_type=F32) + jnp.dot(low, fold, preferred_element_type=F32)
        wide = jnp.concatenate([both] * repeat, axis=1)
        return jnp.sum(jnp.where(diag, wide, 0.0), axis=0, keepdims=True)

    occ_flat = flatten(zmat, fold_major)
    vir_flat = flatten(acc, fold_minor)
    slot = iota((own, pairs), 0)
    occ_out[row // own] = occ_out[row // own] + jnp.where(slot == row % own, occ_flat, 0.0)
    vir_acc[home] = vir_acc[home] + jnp.where(slot == block % own, vir_flat, 0.0)

    @pl.when(t == pl.num_programs(0) - 1)
    def _():
        vir_out[...] = vir_acc[...].astype(vir_out.dtype)


def tiles(sizes, rows, owners, blocks, occ, vir, adj, three, n_dev, n_aux):
    count, pairs, naux = three.shape
    own = occ.shape[0] // n_aux
    smem = pl.BlockSpec(memory_space=pltpu.SMEM)
    vmem = pl.BlockSpec(memory_space=pltpu.VMEM)
    return pl.pallas_call(
        functools.partial(tile_kernel, n_aux, own),
        grid=(count,),
        out_shape=(
            jax.ShapeDtypeStruct((n_aux, own, pairs), F32),
            jax.ShapeDtypeStruct((n_dev, own, pairs), BF16),
        ),
        in_specs=[smem] * 4 + [vmem] * 3 + [pl.BlockSpec((1, pairs, naux), lambda t: (t, 0, 0))],
        out_specs=(vmem, vmem),
        scratch_shapes=[pltpu.VMEM((n_dev, own, pairs), F32)],
        compiler_params=pltpu.CompilerParams(vmem_limit_bytes=48 * 1024 * 1024),
        name="tiles",
    )(sizes, rows, owners, blocks, occ, vir, adj, three)


def exchange_kernel(
    n_blk, n_aux, norm, sizes, occ_ref, vir_ref, occ_out, vir_out, occ_got, vir_got, occ_sems, vir_sems
):
    n_dev = n_blk * n_aux
    b = lax.axis_index("blk")
    a = lax.axis_index("aux")
    me = b * n_aux + a
    barrier = pltpu.get_barrier_semaphore()

    def greet(k, carry):
        p = lax.rem(me + k, n_dev)
        pl.semaphore_signal(barrier, inc=1, device_id=(p // n_aux, p % n_aux), device_id_type=MESH)
        return carry

    lax.fori_loop(1, n_dev, greet, 0)
    pl.semaphore_wait(barrier, n_dev - 1)

    trade(n_blk, n_aux, norm, sizes, occ_ref, vir_ref, occ_out, vir_out, occ_got, vir_got, occ_sems, vir_sems)


def trade(n_blk, n_aux, norm, sizes, occ_ref, vir_ref, occ_out, vir_out, occ_got, vir_got, occ_sems, vir_sems):
    n_dev = n_blk * n_aux
    b = lax.axis_index("blk")
    a = lax.axis_index("aux")
    me = b * n_aux + a
    own, pairs = occ_out.shape

    def vir_copy(k, source):
        p = lax.rem(me + k, n_dev)
        return pltpu.make_async_remote_copy(
            src_ref=vir_ref.at[p],
            dst_ref=vir_got.at[source],
            send_sem=vir_sems.at[0, k],
            recv_sem=vir_sems.at[1, source],
            device_id=(p // n_aux, p % n_aux),
            device_id_type=MESH,
        )

    def occ_copy(k, source):
        q = lax.rem(a + k, n_aux)
        return pltpu.make_async_remote_copy(
            src_ref=occ_ref.at[q],
            dst_ref=occ_got.at[source],
            send_sem=occ_sems.at[0, k],
            recv_sem=occ_sems.at[1, source],
            device_id=(b, q),
            device_id_type=MESH,
        )

    def start_vir(k, carry):
        vir_copy(k, me).start()
        return carry

    def start_occ(k, carry):
        occ_copy(k, a).start()
        return carry

    lax.fori_loop(1, n_dev, start_vir, 0)
    lax.fori_loop(1, n_aux, start_occ, 0)

    def take_vir(k, total):
        source = lax.rem(me + k, n_dev)
        vir_copy(k, source).wait_recv()
        return total + vir_got[source].astype(F32)

    def take_occ(k, total):
        source = lax.rem(a + k, n_aux)
        occ_copy(k, source).wait_recv()
        return total + occ_got[source]

    occ_sum = lax.fori_loop(1, n_aux, take_occ, occ_ref[a])
    vir_sum = lax.fori_loop(1, n_dev, take_vir, vir_ref[me].astype(F32))
    lane = iota((1, pairs), 1)
    for r in range(own):
        size = sizes[a * own + r]
        scale = jnp.where((lane // BS < size) & (lane % BS < size), norm, 0.0).astype(F32)
        occ_out[r : r + 1, :] = occ_sum[r : r + 1, :] * scale
        vir_out[r : r + 1, :] = vir_sum[r : r + 1, :] * scale

    def end_vir(k, carry):
        vir_copy(k, me).wait_send()
        return carry

    def end_occ(k, carry):
        occ_copy(k, a).wait_send()
        return carry

    lax.fori_loop(1, n_dev, end_vir, 0)
    lax.fori_loop(1, n_aux, end_occ, 0)


def exchange(sizes, occ, vir, n_blk, n_aux, norm):
    n_dev, own, pairs = vir.shape
    vmem = pl.BlockSpec(memory_space=pltpu.VMEM)
    out = jax.ShapeDtypeStruct((own, pairs), F32)
    return pl.pallas_call(
        functools.partial(exchange_kernel, n_blk, n_aux, norm),
        out_shape=(out, out),
        in_specs=[pl.BlockSpec(memory_space=pltpu.SMEM), vmem, vmem],
        out_specs=(vmem, vmem),
        scratch_shapes=[
            pltpu.VMEM(occ.shape, occ.dtype),
            pltpu.VMEM(vir.shape, vir.dtype),
            pltpu.SemaphoreType.DMA((2, n_aux)),
            pltpu.SemaphoreType.DMA((2, n_dev)),
        ],
        compiler_params=pltpu.CompilerParams(collective_id=1, has_side_effects=True),
        name="exchange",
    )(sizes, occ, vir)


def shards(
    n_blk, n_aux, adjoint, three_centre, occ_density, vir_density, block_sizes, tile_rows, col_owner, col_block
):
    n_dev = n_blk * n_aux
    count = three_centre.shape[0]
    naux = three_centre.shape[3]
    own = occ_density.shape[0] // n_aux
    depth = adjoint.shape[0]
    three = three_centre.reshape(count, BS * BS, naux)
    if n_aux == 4 and n_blk % 2 == 0:
        both = fused(
            block_sizes, tile_rows, col_owner.reshape(count), col_block, adjoint, occ_density, vir_density,
            three, n_blk, n_aux, naux ** -0.5,
        )
        return both[0], both[1]
    aux_here = lax.axis_index("aux")
    own_sizes = lax.dynamic_slice_in_dim(block_sizes, aux_here * own, own, 0)
    own_vir = lax.dynamic_slice_in_dim(vir_density, aux_here * own, own, 0)
    lane = jnp.arange(BS * BS, dtype=jnp.int32)[None, :]
    inside = (lane // BS < own_sizes[:, None]) & (lane % BS < own_sizes[:, None])
    own_vir = jnp.where(inside, own_vir, jnp.zeros_like(own_vir))
    got = lax.all_gather(jnp.concatenate((adjoint, own_vir), axis=0), ("blk", "aux"), axis=0)
    adj = got[:, :depth, :].reshape(naux, naux)
    vir = got[:, depth:, :]
    occ_terms, vir_terms = tiles(
        block_sizes, tile_rows, col_owner.reshape(count), col_block, occ_density, vir, adj,
        three, n_dev, n_aux,
    )
    return exchange(block_sizes, occ_terms, vir_terms, n_blk, n_aux, naux ** -0.5)


def solution(mesh):
    in_specs = (
        P(("blk", "aux"), None),
        P(("blk", "aux"), None, None, None),
        P("blk", None),
        P("blk", None),
        P("blk"),
        P(("blk", "aux")),
        P(("blk", "aux"), None),
        P(("blk", "aux")),
    )
    out_specs = (P(("blk", "aux"), None), P(("blk", "aux"), None))
    body = functools.partial(shards, mesh.shape["blk"], mesh.shape["aux"])
    return jax.shard_map(body, mesh=mesh, in_specs=in_specs, out_specs=out_specs, check_vma=False)
```

profile of v0, /device:TPU:0, one launch (start us, length us, event | category | flops | bytes accessed | tf_op | source)
XLA Modules:
  0.0 54.4 jit_solution(15237679386088295038)
XLA Ops:
  0.6 52.4 %fused.1 = f32[2,2,1024]{2,1,0:T(2,128)} custom-call(s32[8]{0:T(128)} %sizes.1, s32[4]{0:T(128)} %rows.1, s32[4]{0:T(128)} %bitcast.7, s32[4]{0:T(128)} %blocks.1, bf16[32,1024]{1,0:T(8,128)(2,1)} %adj_ref.1, bf16[8,1024]{1,0:T(8,128)(2,1)} %occ_ref.1, bf16[8,1024]{1,0:T(8,128)(2,1)} %vir_ref.1, bf16[4,1024,1024]{2,1,0:T(8,128)(2,1)} %bitcast.6), custom_call_target="tpu_custom_call" | custom-call | tf_op jit(solution)/shard_map/fused/pallas_call | solution.py:296
  53.1 1.3 %slice_bitcast_fusion = (f32[2,1024]{1,0:T(2,128)}, f32[2,1024]{1,0:T(2,128)}) fusion(f32[2,2,1024]{2,1,0:T(2,128)} %fused.1), kind=kLoop, calls=%fused_computation | loop fusion | bytes 32768 | tf_op jit(solution)/shard_map/squeeze | solution.py:536
where the time goes:
time: 54.6 us; the launch traced here: 54.4 us
  Pallas kernels  52.4 us (96%)
  local copies, waits for them, and re-layouts  1.32 us (2%)
  between operations  0.64 us (1%)
    pallas_call x1, Pallas kernels, fused(): pl.pallas_call(functools.partial(fused_kernel, n_blk, n_aux, norm), out_s...  52.4 us
    squeeze x1, local copies, waits for them, and re-layouts, shards(): return (both[0], both[1])  1.32 us

commit v1 on v0

--- a/solution.py
+++ b/solution.py
@@ -8,6 +8,7 @@
 from jax.sharding import PartitionSpec as P
 
 BS = 32
+SUB = 8
 CHUNK = 256
 MESH = pl.DeviceIdType.MESH
 F32 = jnp.float32
@@ -18,12 +19,6 @@
     return lax.broadcasted_iota(jnp.int32, shape, dim)
 
 
-def fold(minor, pairs):
-    index = iota((pairs, 128), 0)
-    index = index % BS if minor else index // BS
-    return (index == iota((pairs, 128), 1) % BS).astype(BF16)
-
-
 def dot(left, right):
     return jnp.dot(left, right, preferred_element_type=F32)
 
@@ -32,32 +27,53 @@
     return lax.dot_general(left, right, (((1,), (1,)), ((), ())), preferred_element_type=F32)
 
 
+def fold(rows, lanes, row_key, lane_key):
+    return (row_key(iota((rows, lanes), 0)) == lane_key(iota((rows, lanes), 1))).astype(BF16)
+
+
+def exact(mat, folding):
+    high = mat.astype(BF16)
+    low = (mat - high.astype(F32)).astype(BF16)
+    return dot(high, folding) + dot(low, folding)
+
+
+def minor(index):
+    return index % BS
+
+
+def inner(index):
+    return index // (SUB * SUB) * SUB + index % SUB
+
+
+def outer(index):
+    return index // SUB
+
+
 def fused_kernel(
     n_blk, n_aux, norm,
-    sizes, rows, owners, blocks, adj_ref, occ_ref, vir_ref, t_hbm,
+    sizes, rows, owners, blocks, adj_hbm, occ_ref, vir_ref, t_hbm,
     out_ref,
-    got, tbuf, cbuf, occ_rep, vir_rep, occ_sums, vir_sums, occ_send, vir_send, occ_got, vir_got,
-    t_sem, send_sem, recv_sem, occ_sems, vir_sems,
+    got, tbuf, cbuf, rbuf, ybuf, vir_send, vir_got, occ_send, occ_got,
+    adj_sem, t_sem, near_sem, recv_sem, send_sem, trade_sem,
 ):
     n_dev = n_blk * n_aux
-    occ_out, vir_out = out_ref.at[0], out_ref.at[1]
     depth = n_blk // 2
-    count, pairs, naux = tbuf.shape
-    own = occ_out.shape[0]
-    arows = adj_ref.shape[0]
+    count, groups, _, _, naux = tbuf.shape
+    pairs = BS * BS
+    wide = BS * SUB
+    own = out_ref.shape[1]
+    arows = adj_hbm.shape[0]
+    half = arows // 2
     span = naux // depth
     per_plane = n_dev // depth
     b = lax.axis_index("blk")
     a = lax.axis_index("aux")
     z, y, x, c = b // 2, b % 2, a // 2, a % 2
-    up, down, over_x, over_y, mate = range(5)
-    place = {
-        up: (b + 2, a),
-        down: (b - 2, a),
-        over_x: (b, (1 - x) * 2 + c),
-        over_y: (z * 2 + 1 - y, a),
-        mate: (b, x * 2 + 1 - c),
-    }
+    col, sides, corner, mates = range(4)
+    over_x = (b, (1 - x) * 2 + c)
+    over_y = (z * 2 + 1 - y, a)
+    mate = (b, x * 2 + 1 - c)
+    above, below = (b + 2, a), (b - 2, a)
     has_up, has_down = z < depth - 1, z > 0
     me = b * n_aux + a
 
@@ -66,261 +82,305 @@
 
     barrier = pltpu.get_barrier_semaphore()
 
-    def greet(k, carry):
-        p = lax.rem(me + k, n_dev)
-        pl.semaphore_signal(barrier, inc=1, device_id=(p // n_aux, p % n_aux), device_id_type=MESH)
-        return carry
-
-    lax.fori_loop(1, n_dev, greet, 0)
-    fetches = [pltpu.make_async_copy(t_hbm.at[t], tbuf.at[t], t_sem.at[t]) for t in range(count)]
-    for fetch in fetches:
-        fetch.start()
+    def tell(sem, device):
+        pl.semaphore_signal(sem, inc=1, device_id=device, device_id_type=MESH)
+
+    for device in (over_x, over_y, mate):
+        tell(barrier, device)
+    pl.when(has_up)(lambda: tell(barrier, above))
+    pl.when(has_down)(lambda: tell(barrier, below))
+
+    adj_copy = pltpu.make_async_copy(adj_hbm, got.at[me, pl.ds(0, arows)], adj_sem)
+    adj_copy.start()
+    for t in range(count):
+        for g in range(groups):
+            pltpu.make_async_copy(t_hbm.at[t, :, g], tbuf.at[t, g], t_sem.at[t]).start()
 
     lane = iota((1, pairs), 1)
-    major, minor = lane // BS, lane % BS
-    got[me, :arows, :] = adj_ref[...]
+    diag = iota((BS, pairs), 1) // BS == iota((BS, pairs), 0)
+
+    def live(size):
+        return (lane // BS < size) & (lane % BS < size)
+
+    def pick(all_rows, at):
+        return jnp.sum(jnp.where(iota(all_rows.shape, 0) == at, all_rows, 0.0), axis=0, keepdims=True)
+
     vir_all = vir_ref[...].astype(F32)
-    slot = iota(vir_all.shape, 0)
-    mine = []
-    for r in range(own):
-        size = sizes[a * own + r]
-        row = jnp.sum(jnp.where(slot == a * own + r, vir_all, 0.0), axis=0, keepdims=True)
-        mine.append(jnp.where((major < size) & (minor < size), row, 0.0))
+    mine = [jnp.where(live(sizes[a * own + r]), pick(vir_all, a * own + r), 0.0) for r in range(own)]
     got[me, arows:, :] = jnp.concatenate(mine, axis=0).astype(BF16)
 
-    diag = iota((BS, pairs), 1) // BS == iota((BS, pairs), 0)
-    fold_minor = fold(True, pairs)
-    pl.semaphore_wait(barrier, n_dev - 1)
-
-    def copy(way, block):
-        return pltpu.make_async_remote_copy(
-            src_ref=got.at[block],
-            dst_ref=got.at[block],
-            send_sem=send_sem.at[way, block],
-            recv_sem=recv_sem.at[block],
-            device_id=place[way],
+    adj_copy.wait()
+    pl.semaphore_wait(barrier, 3 + has_up.astype(jnp.int32) + has_down.astype(jnp.int32))
+
+    def send(block, device, kind, zz, part=None):
+        ref = got.at[block] if part is None else got.at[block, part]
+        pltpu.make_async_remote_copy(
+            src_ref=ref,
+            dst_ref=ref,
+            send_sem=send_sem,
+            recv_sem=recv_sem.at[kind, zz],
+            device_id=device,
             device_id_type=MESH,
-        )
-
-    def send(way, block, when=None):
-        if when is None:
-            copy(way, block).start()
-        else:
-
-            @pl.when(when)
-            def _():
-                copy(way, block).start()
-
-    def arrive(block):
-        copy(mate, block).wait_recv()
-
-    send(up, me, has_up)
-    send(down, me, has_down)
-    send(over_x, me)
-    send(over_y, me)
-    send(mate, me)
+        ).start()
+
+    def arrive(kind, zz, number):
+        part = got.at[pl.ds(0, number)]
+        pltpu.make_async_copy(part, part, recv_sem.at[kind, zz]).wait()
+
+    for device in (over_x, over_y):
+        send(me, device, sides, z)
+    pl.when(has_up)(lambda: send(me, above, col, z))
+    pl.when(has_down)(lambda: send(me, below, col, z))
+    send(me, mate, mates, z)
+
+    def reach(hop):
+        pl.when(has_down & (z + hop < depth))(lambda: tell(near_sem.at[0], below))
+        pl.when(has_up & (z - hop >= 0))(lambda: tell(near_sem.at[1], above))
+
+        @pl.when(z + hop + 1 < depth)
+        def _():
+            pl.semaphore_wait(near_sem.at[0], 1)
+            send(me, (b + 2 * (hop + 1), a), col, z)
+
+        @pl.when(z - hop - 1 >= 0)
+        def _():
+            pl.semaphore_wait(near_sem.at[1], 1)
+            send(me, (b - 2 * (hop + 1), a), col, z)
+
+    def relay_col(zz):
+        block = ident(x, y, zz, c)
+        arrive(col, zz, 1)
+        send(block, over_x, sides, zz)
+        send(block, over_y, sides, zz)
+        send(block, mate, mates, zz)
+
+    def relay_sides(zz):
+        arrive(sides, zz, 2)
+        block_x, block_y = ident(1 - x, y, zz, c), ident(x, 1 - y, zz, c)
+        send(block_x, over_y, corner, zz, pl.ds(0, half))
+        send(block_y, over_x, corner, zz, pl.ds(half, arows + own - half))
+        send(block_x, mate, mates, zz)
+        send(block_y, mate, mates, zz)
+
+    def relay_corner(zz):
+        arrive(corner, zz, 1)
+        send(ident(1 - x, 1 - y, zz, c), mate, mates, zz)
+
+    low = z < depth // 2
+    zl = jnp.where(low, z, depth - 1 - z)
+
+    def plane(k):
+        near = zl + k // 2 if k % 2 == 0 else zl - (k + 1) // 2
+        at = jnp.where(k <= 2 * zl, near, k)
+        return jnp.where(low, at, depth - 1 - at)
+
+    order = [plane(k) for k in range(depth)]
 
     occ_all = occ_ref[...].astype(F32)
     parts = []
     for t in range(count):
-        size = sizes[rows[t]]
-        row = jnp.sum(jnp.where(slot == rows[t], occ_all, 0.0), axis=0, keepdims=True)
-        row = jnp.where((major < size) & (minor < size), row, 0.0)
+        row = jnp.where(live(sizes[rows[t]]), pick(occ_all, rows[t]), 0.0)
         parts.append(jnp.where(diag, row, 0.0))
-    spread = (iota((128, pairs), 0) == iota((128, pairs), 1) // BS).astype(BF16)
-    square = dot(jnp.concatenate(parts, axis=0).astype(BF16), fold_minor)
-    occ_rep[...] = dot(square.astype(BF16), spread).reshape(occ_rep.shape)
-
-    def column(zz, from_up):
-        block = ident(x, y, zz, c)
-        arrive(block)
-        if from_up:
-            send(down, block, has_down)
-        else:
-            send(up, block, has_up)
-        send(over_x, block)
-        send(over_y, block)
-        send(mate, block)
-
-    def sides(zz, _):
-        block = ident(1 - x, y, zz, c)
-        arrive(block)
-        send(over_y, block, zz % 2 == 0)
-        send(mate, block)
-        block = ident(x, 1 - y, zz, c)
-        arrive(block)
-        send(over_x, block, zz % 2 == 1)
-        send(mate, block)
-
-    def corner(zz, _):
-        block = ident(1 - x, 1 - y, zz, c)
-        arrive(block)
-        send(mate, block)
-
-    def mates(zz, _):
-        for xx in (x, 1 - x):
-            for yy in (y, 1 - y):
-                arrive(ident(xx, yy, zz, 1 - c))
-
-    def contract(zz, first, last):
+    square = dot(jnp.concatenate(parts, axis=0).astype(BF16), fold(pairs, wide, minor, outer))
+    same_sub = iota((wide, wide), 0) % SUB == iota((wide, wide), 1) % SUB
+
+    def rotate(t):
+        spread = jnp.broadcast_to(square[t * BS : (t + 1) * BS][:, None, :], (BS, SUB, wide)).reshape(wide, wide)
+        left = jnp.where(same_sub, spread, 0.0).astype(BF16)
+        pltpu.make_async_copy(tbuf.at[t], tbuf.at[t], t_sem.at[t]).wait()
+        for g in range(groups):
+            rbuf[t, g] = dot(left, tbuf[t, g].reshape(wide, naux)).astype(BF16).reshape(BS, SUB, naux)
+
+    def contract(k, t):
+        zz = order[k]
         part = got[pl.ds(zz * per_plane, per_plane), :arows, :].reshape(span, naux)
         columns = pl.ds(pl.multiple_of(zz * span, span), span)
-
-        def step(t, carry):
-            cbuf[t, :, columns] = dot_nt(tbuf[t], part).astype(BF16)
-            return carry
-
-        lax.fori_loop(first, last, step, 0)
-
-    def planes(dist, work):
-        if dist == 0:
-            work(z, None)
-        elif dist < depth:
-
-            @pl.when(z + dist < depth)
-            def _():
-                work(z + dist, True)
-
-            @pl.when(z - dist >= 0)
-            def _():
-                work(z - dist, False)
-
-    def whole(zz, _):
-        mates(zz, _)
-        contract(zz, 0, count)
-
-    planes(1, column)
-    planes(0, sides)
-    planes(2, column)
-    planes(1, sides)
-    planes(0, corner)
-    for fetch in fetches:
-        fetch.wait()
-    mates(z, None)
-    contract(z, 0, count // 2)
-    planes(3, column)
-    contract(z, count // 2, count)
-    for dist in range(1, depth):
-        planes(dist, corner)
-        planes(dist + 1, sides)
-        planes(dist, whole)
-        planes(dist + 3, column)
+        new = dot_nt(tbuf[t].reshape(pairs, naux), part).astype(BF16)
+        cbuf[t, :, :, :, columns] = new.reshape(groups, BS, SUB, span)
+
+    events = {
+        (0, 1): [lambda: relay_sides(order[1])],
+        (0, 3): [lambda: relay_col(order[3])],
+        (1, 0): [lambda: relay_sides(order[2]), lambda: relay_corner(order[1]), lambda: arrive(mates, order[1], 4)],
+        (1, 1): [lambda: relay_corner(order[2])],
+        (1, 3): [lambda: relay_sides(order[3])],
+        (2, 0): [lambda: arrive(mates, order[2], 4)],
+        (2, 2): [lambda: relay_corner(order[3])],
+        (3, 0): [lambda: arrive(mates, order[3], 4)],
+    }
+
+    rotate(0)
+    reach(1)
+    rotate(1)
+    reach(2)
+    rotate(2)
+    rotate(3)
+    relay_sides(order[0])
+    relay_col(order[1])
+    relay_corner(order[0])
+    relay_col(order[2])
+    arrive(mates, order[0], 4)
+    for k in range(depth):
+        for t in range(count):
+            for event in events.get((k, t), []):
+                event()
+            contract(k, t)
+
+    same_row = iota((SUB, SUB, wide), 0) == iota((SUB, SUB, wide), 2) % (SUB * SUB) // SUB
+    lanes_of = iota((SUB, 128), 1) // BS
+
+    def compact(square):
+        total = jnp.zeros((SUB, 128), F32)
+        for g in range(groups):
+            total = jnp.where(lanes_of == g, square[g * SUB : (g + 1) * SUB], total)
+        return total
+
+    parts = []
+    for t in range(count):
+        acc = jnp.zeros((wide, wide), F32)
+        for at in range(0, BS, SUB):
+            left = cbuf[t, :, at : at + SUB].reshape(wide, naux)
+            acc = acc + dot_nt(left, rbuf[t, :, at : at + SUB].reshape(wide, naux))
+        acc = jnp.where(same_row, acc.reshape(groups, SUB, SUB, wide), 0.0)
+        parts.append(jnp.sum(acc, axis=1).reshape(BS, wide))
+    both = exact(jnp.concatenate(parts, axis=0), fold(wide, 128, inner, minor))
+    terms = [compact(both[t * BS : (t + 1) * BS]) for t in range(count)]
+    for p in range(n_dev):
+        slots = []
+        for r in range(own):
+            total = jnp.zeros((SUB, 128), F32)
+            for t in range(count):
+                here = owners[t] * (n_aux * own) + blocks[t] == p * own + r
+                total = total + jnp.where(here, terms[t], 0.0)
+            slots.append(total)
+        vir_send[p] = jnp.concatenate(slots, axis=0).astype(BF16)
+    vir_got[me] = vir_send[me]
+
+    def send_vir(k, carry):
+        p = lax.rem(me + k, n_dev)
+        pltpu.make_async_remote_copy(
+            src_ref=vir_send.at[p],
+            dst_ref=vir_got.at[me],
+            send_sem=trade_sem.at[0],
+            recv_sem=trade_sem.at[1],
+            device_id=(p // n_aux, p % n_aux),
+            device_id_type=MESH,
+        ).start()
+        return carry
+
+    lax.fori_loop(1, n_dev, send_vir, 0)
 
     parts = []
     for t in range(count):
         home = owners[t] * n_aux + blocks[t] // own
-        near = got[home, arows:, :].astype(F32)
-        row = jnp.sum(jnp.where(iota(near.shape, 0) == blocks[t] % own, near, 0.0), axis=0, keepdims=True)
+        row = pick(got[home, arows:, :].astype(F32), blocks[t] % own)
         parts.append(jnp.where(diag, row, 0.0))
-    square = dot(jnp.concatenate(parts, axis=0).astype(BF16), fold_minor)
-    vir_rep[...] = jnp.concatenate([square] * (pairs // 128), axis=1).reshape(vir_rep.shape)
-
-    def tile(t, carry):
-        acc = jnp.zeros((BS, pairs), F32)
-        lines = []
-        for first in range(0, pairs, CHUNK):
-            gram = dot_nt(cbuf[t, first : first + CHUNK, :], tbuf[t])
-            for at in range(CHUNK // BS):
-                i = first // BS + at
-                block_i = gram[at * BS : (at + 1) * BS, :]
-                acc = acc + block_i * occ_rep[t, i : i + 1, :]
-                lines.append(jnp.sum(block_i * vir_rep[t], axis=0, keepdims=True))
-        vir_sums[t] = acc
-        occ_sums[t] = jnp.concatenate(lines, axis=0)
-        return carry
-
-    lax.fori_loop(0, count, tile, 0)
-
-    def flatten(mat, folding):
-        high = mat.astype(BF16)
-        low = (mat - high.astype(F32)).astype(BF16)
-        both = dot(high, folding) + dot(low, folding)
-        lines = []
-        for t in range(count):
-            wide = jnp.concatenate([both[t * BS : (t + 1) * BS]] * (pairs // 128), axis=1)
-            lines.append(jnp.sum(jnp.where(diag, wide, 0.0), axis=0, keepdims=True))
-        return lines
-
-    vir_flat = flatten(vir_sums[...].reshape(count * BS, pairs), fold_minor)
-    shape = (n_dev, own, 1)
-    place_id = iota(shape, 0) * own + iota(shape, 1)
-    total = jnp.zeros(vir_send.shape, F32)
+    square_v = dot(jnp.concatenate(parts, axis=0).astype(BF16), fold(pairs, wide, minor, inner))
     for t in range(count):
-        hot = (place_id == owners[t] * (n_aux * own) + blocks[t]).astype(F32)
-        total = total + hot * vir_flat[t].reshape(1, 1, pairs)
-    vir_send[...] = total.astype(BF16)
-    occ_flat = flatten(occ_sums[...].reshape(count * BS, pairs), fold(False, pairs))
-    shape = (n_aux, own, 1)
-    place_id = iota(shape, 0) * own + iota(shape, 1)
-    total = jnp.zeros(occ_send.shape, F32)
+        spread = square_v[t * BS : (t + 1) * BS].reshape(groups, 1, SUB, wide)
+        spread = jnp.broadcast_to(spread, (groups, SUB, SUB, wide))
+        left = jnp.where(same_row, spread, 0.0).reshape(wide, wide).astype(BF16)
+        for at in range(0, BS, SUB):
+            new = dot(left, tbuf[t, :, at : at + SUB].reshape(wide, naux)).astype(BF16)
+            ybuf[t, :, at : at + SUB] = new.reshape(groups, SUB, SUB, naux)
+
+    gather = fold(BS, wide, lambda index: index, outer)
+    parts = []
     for t in range(count):
-        hot = (place_id == rows[t]).astype(F32)
-        total = total + hot * occ_flat[t].reshape(1, 1, pairs)
-    occ_send[...] = total
-
-    trade(
-        n_blk, n_aux, norm, sizes, occ_send, vir_send, occ_out, vir_out, occ_got, vir_got, occ_sems, vir_sems
-    )
-
-    for zz in range(depth):
-        block = ident(x, y, zz, c)
-        for way in (over_x, over_y, mate):
-            copy(way, block).wait_send()
-
-        @pl.when((zz <= z) & has_up)
-        def _():
-            copy(up, ident(x, y, zz, c)).wait_send()
-
-        @pl.when((zz >= z) & has_down)
-        def _():
-            copy(down, ident(x, y, zz, c)).wait_send()
-
-        block = ident(1 - x, y, zz, c)
-        copy(mate, block).wait_send()
-        if zz % 2 == 0:
-            copy(over_y, block).wait_send()
-        block = ident(x, 1 - y, zz, c)
-        copy(mate, block).wait_send()
-        if zz % 2 == 1:
-            copy(over_x, block).wait_send()
-        copy(mate, ident(1 - x, 1 - y, zz, c)).wait_send()
+        acc = jnp.zeros((wide, wide), F32)
+        for g in range(groups):
+            acc = acc + dot_nt(cbuf[t, g].reshape(wide, naux), ybuf[t, g].reshape(wide, naux))
+        acc = jnp.where(same_sub, acc, 0.0)
+        high = acc.astype(BF16)
+        parts.append(dot(gather, high) + dot(gather, (acc - high.astype(F32)).astype(BF16)))
+    both = exact(jnp.concatenate(parts, axis=0), fold(wide, 128, outer, minor))
+    terms = [compact(both[t * BS : (t + 1) * BS]) for t in range(count)]
+    for q in range(n_aux):
+        slots = []
+        for r in range(own):
+            total = jnp.zeros((SUB, 128), F32)
+            for t in range(count):
+                total = total + jnp.where(rows[t] == q * own + r, terms[t], 0.0)
+            slots.append(total)
+        occ_send[q] = jnp.concatenate(slots, axis=0)
+    occ_got[a] = occ_send[a]
+    for k in range(1, n_aux):
+        q = lax.rem(a + k, n_aux)
+        pltpu.make_async_remote_copy(
+            src_ref=occ_send.at[q],
+            dst_ref=occ_got.at[a],
+            send_sem=trade_sem.at[2],
+            recv_sem=trade_sem.at[3],
+            device_id=(b, q),
+            device_id_type=MESH,
+        ).start()
+
+    def done(ref, sem):
+        pltpu.make_async_copy(ref, ref, sem).wait()
+
+    done(vir_got.at[pl.ds(0, n_dev - 1)], trade_sem.at[1])
+    vir_sum = jnp.sum(vir_got[...].astype(F32), axis=0)
+    done(occ_got.at[pl.ds(0, n_aux - 1)], trade_sem.at[3])
+    occ_sum = jnp.sum(occ_got[...], axis=0)
+
+    sums = jnp.concatenate([occ_sum, vir_sum], axis=0)
+    lanes_all = iota(sums.shape, 1) // BS
+    parts = [jnp.where(lanes_all == g, sums, 0.0) for g in range(groups)]
+    both = exact(jnp.concatenate(parts, axis=0), fold(128, 128, minor, minor))
+    both = both.reshape(groups, 2 * own, SUB, 128)
+    per_tile = 128 // BS
+    lines = []
+    for m in range(pairs // 128):
+        first = m * per_tile
+        here = iota((SUB, 128), 0) == first % SUB + lanes_of
+        lines.append(jnp.sum(jnp.where(here, both[first // SUB], 0.0), axis=1))
+    flat = jnp.concatenate(lines, axis=1)
+    for r in range(own):
+        scale = jnp.where(live(sizes[a * own + r]), norm, 0.0).astype(F32)
+        out_ref[0, r : r + 1, :] = flat[r : r + 1, :] * scale
+        out_ref[1, r : r + 1, :] = flat[own + r : own + r + 1, :] * scale
+
+    done(vir_send.at[pl.ds(0, n_dev - 1)], trade_sem.at[0])
+    done(occ_send.at[pl.ds(0, n_aux - 1)], trade_sem.at[2])
+    done(got.at[pl.ds(0, depth - 1 + 7 * depth)], send_sem)
 
 
 def fused(sizes, rows, owners, blocks, adj, occ, vir, three, n_blk, n_aux, norm):
     n_dev = n_blk * n_aux
-    count, pairs, naux = three.shape
+    count, naux = three.shape[0], three.shape[3]
     own = occ.shape[0] // n_aux
+    groups = BS // SUB
     smem = pl.BlockSpec(memory_space=pltpu.SMEM)
     vmem = pl.BlockSpec(memory_space=pltpu.VMEM)
-    square = pltpu.VMEM((count, BS, pairs), F32)
+    hbm = pl.BlockSpec(memory_space=pl.ANY)
+    tile = pltpu.VMEM((count, groups, BS, SUB, naux), BF16)
     return pl.pallas_call(
         functools.partial(fused_kernel, n_blk, n_aux, norm),
-        out_shape=jax.ShapeDtypeStruct((2, own, pairs), F32),
-        in_specs=[smem] * 4 + [vmem] * 3 + [pl.BlockSpec(memory_space=pl.ANY)],
+        out_shape=jax.ShapeDtypeStruct((2, own, BS * BS), F32),
+        in_specs=[smem] * 4 + [hbm, vmem, vmem, hbm],
         out_specs=vmem,
         scratch_shapes=[
             pltpu.VMEM((n_dev, adj.shape[0] + own, naux), BF16),
-            pltpu.VMEM((count, pairs, naux), BF16),
-            pltpu.VMEM((count, pairs, naux), BF16),
-            square,
-            square,
-            square,
-            square,
-            pltpu.VMEM((n_aux, own, pairs), F32),
-            pltpu.VMEM((n_dev, own, pairs), BF16),
-            pltpu.VMEM((n_aux, own, pairs), F32),
-            pltpu.VMEM((n_dev, own, pairs), BF16),
+            tile,
+            tile,
+            tile,
+            tile,
+            pltpu.VMEM((n_dev, own * SUB, 128), BF16),
+            pltpu.VMEM((n_dev, own * SUB, 128), BF16),
+            pltpu.VMEM((n_aux, own * SUB, 128), F32),
+            pltpu.VMEM((n_aux, own * SUB, 128), F32),
+            pltpu.SemaphoreType.DMA,
             pltpu.SemaphoreType.DMA((count,)),
-            pltpu.SemaphoreType.DMA((5, n_dev)),
-            pltpu.SemaphoreType.DMA((n_dev,)),
-            pltpu.SemaphoreType.DMA((2, n_aux)),
-            pltpu.SemaphoreType.DMA((2, n_dev)),
+            pltpu.SemaphoreType.REGULAR((2,)),
+            pltpu.SemaphoreType.DMA((4, n_blk // 2)),
+            pltpu.SemaphoreType.DMA,
+            pltpu.SemaphoreType.DMA((4,)),
         ],
         compiler_params=pltpu.CompilerParams(
             collective_id=0, has_side_effects=True, vmem_limit_bytes=67043328
         ),
         name="fused",
-    )(sizes, rows, owners, blocks, adj, occ, vir, three)
+    )(sizes, rows, owners, blocks, adj, occ, vir, three.reshape(count, BS, groups, SUB, naux))
 
 
 def tile_kernel(
@@ -528,10 +588,10 @@
     own = occ_density.shape[0] // n_aux
     depth = adjoint.shape[0]
     three = three_centre.reshape(count, BS * BS, naux)
-    if n_aux == 4 and n_blk % 2 == 0:
+    if n_aux == 4 and n_blk == 8:
         both = fused(
             block_sizes, tile_rows, col_owner.reshape(count), col_block, adjoint, occ_density, vir_density,
-            three, n_blk, n_aux, naux ** -0.5,
+            three_centre, n_blk, n_aux, naux ** -0.5,
         )
         return both[0], both[1]
     aux_here = lax.axis_index("aux")

time: 54.6 us -> 49.2 us (0.901)
  Pallas kernels: 52.4 us -> 46.9 us
    pallas_call x1, Pallas kernels: 52.4 us -> 46.9 us  [fused(): pl.pallas_call(functools.partial(fused_kernel, n_blk, n_aux, norm), out_s...]
where the time goes in v1:
time: 49.2 us; the launch traced here: 48.8 us
  Pallas kernels  46.9 us (95%)
  local copies, waits for them, and re-layouts  1.32 us (3%)
  between operations  0.64 us (1%)
    pallas_call x1, Pallas kernels, fused(): pl.pallas_call(functools.partial(fused_kernel, n_blk, n_aux, norm), out_s...  46.9 us
    squeeze x1, local copies, waits for them, and re-layouts, shards(): return (both[0], both[1])  1.32 us

profile of v1, /device:TPU:0, one launch (start us, length us, event | category | flops | bytes accessed | tf_op | source)
XLA Modules:
  0.0 48.8 jit_solution(2669293579394642719)
XLA Ops:
  0.6 46.9 %fused.1 = f32[2,2,1024]{2,1,0:T(2,128)} custom-call(s32[8]{0:T(128)} %sizes.1, s32[4]{0:T(128)} %rows.1, s32[4]{0:T(128)} %bitcast.7, s32[4]{0:T(128)} %blocks.1, bf16[32,1024]{1,0:T(8,128)(2,1)} %adj_hbm.1, bf16[8,1024]{1,0:T(8,128)(2,1)} %occ_ref.1, bf16[8,1024]{1,0:T(8,128)(2,1)} %vir_ref.1, bf16[4,32,4,8,1024]{4,3,2,1,0:T(8,128)(2,1)} %bitcast.6), custom_call_target="tpu_custom_call" | custom-call | tf_op jit(solution)/shard_map/fused/pallas_call | solution.py:357
  47.5 1.3 %slice_bitcast_fusion = (f32[2,1024]{1,0:T(2,128)}, f32[2,1024]{1,0:T(2,128)}) fusion(f32[2,2,1024]{2,1,0:T(2,128)} %fused.1), kind=kLoop, calls=%fused_computation | loop fusion | bytes 32768 | tf_op jit(solution)/shard_map/squeeze | solution.py:596

commit v2 on v1

--- a/solution.py
+++ b/solution.py
@@ -51,10 +51,10 @@
 
 def fused_kernel(
     n_blk, n_aux, norm,
-    sizes, rows, owners, blocks, adj_hbm, occ_ref, vir_ref, t_hbm,
+    sizes_hbm, rows_hbm, owners_hbm, blocks_hbm, adj_hbm, occ_hbm, vir_hbm, t_hbm,
     out_ref,
-    got, tbuf, cbuf, rbuf, ybuf, vir_send, vir_got, occ_send, occ_got,
-    adj_sem, t_sem, near_sem, recv_sem, send_sem, trade_sem,
+    sizes, rows, owners, blocks, occ_ref, vir_ref, got, tbuf, cbuf, rbuf, ybuf, vir_send, vir_got, occ_send, occ_got,
+    in_sem, t_sem, near_sem, recv_sem, send_sem, trade_sem,
 ):
     n_dev = n_blk * n_aux
     depth = n_blk // 2
@@ -90,26 +90,32 @@
     pl.when(has_up)(lambda: tell(barrier, above))
     pl.when(has_down)(lambda: tell(barrier, below))
 
-    adj_copy = pltpu.make_async_copy(adj_hbm, got.at[me, pl.ds(0, arows)], adj_sem)
-    adj_copy.start()
+    pairs_in = (
+        (vir_hbm, vir_ref), (sizes_hbm, sizes), (adj_hbm, got.at[me, pl.ds(0, arows)]),
+        (rows_hbm, rows), (occ_hbm, occ_ref), (owners_hbm, owners), (blocks_hbm, blocks),
+    )
+    fetches = [pltpu.make_async_copy(src, dst, in_sem.at[i]) for i, (src, dst) in enumerate(pairs_in)]
+    for fetch in fetches:
+        fetch.start()
+
+    lane = iota((1, pairs), 1)
+    diag = iota((BS, pairs), 1) // BS == iota((BS, pairs), 0)
+
+    def live(size):
+        return (lane // BS < size) & (lane % BS < size)
+
+    def pick(all_rows, at):
+        return jnp.sum(jnp.where(iota(all_rows.shape, 0) == at, all_rows, 0.0), axis=0, keepdims=True)
+
+    for fetch in fetches:
+        fetch.wait()
     for t in range(count):
         for g in range(groups):
             pltpu.make_async_copy(t_hbm.at[t, :, g], tbuf.at[t, g], t_sem.at[t]).start()
-
-    lane = iota((1, pairs), 1)
-    diag = iota((BS, pairs), 1) // BS == iota((BS, pairs), 0)
-
-    def live(size):
-        return (lane // BS < size) & (lane % BS < size)
-
-    def pick(all_rows, at):
-        return jnp.sum(jnp.where(iota(all_rows.shape, 0) == at, all_rows, 0.0), axis=0, keepdims=True)
-
     vir_all = vir_ref[...].astype(F32)
     mine = [jnp.where(live(sizes[a * own + r]), pick(vir_all, a * own + r), 0.0) for r in range(own)]
     got[me, arows:, :] = jnp.concatenate(mine, axis=0).astype(BF16)
 
-    adj_copy.wait()
     pl.semaphore_wait(barrier, 3 + has_up.astype(jnp.int32) + has_down.astype(jnp.int32))
 
     def send(block, device, kind, zz, part=None):
@@ -133,10 +139,11 @@
     pl.when(has_down)(lambda: send(me, below, col, z))
     send(me, mate, mates, z)
 
-    def reach(hop):
+    def report(hop):
         pl.when(has_down & (z + hop < depth))(lambda: tell(near_sem.at[0], below))
         pl.when(has_up & (z - hop >= 0))(lambda: tell(near_sem.at[1], above))
 
+    def reach(hop):
         @pl.when(z + hop + 1 < depth)
         def _():
             pl.semaphore_wait(near_sem.at[0], 1)
@@ -176,6 +183,7 @@
 
     order = [plane(k) for k in range(depth)]
 
+    report(1)
     occ_all = occ_ref[...].astype(F32)
     parts = []
     for t in range(count):
@@ -194,9 +202,8 @@
     def contract(k, t):
         zz = order[k]
         part = got[pl.ds(zz * per_plane, per_plane), :arows, :].reshape(span, naux)
-        columns = pl.ds(pl.multiple_of(zz * span, span), span)
         new = dot_nt(tbuf[t].reshape(pairs, naux), part).astype(BF16)
-        cbuf[t, :, :, :, columns] = new.reshape(groups, BS, SUB, span)
+        cbuf[t, zz] = new.reshape(groups, BS, SUB, span)
 
     events = {
         (0, 1): [lambda: relay_sides(order[1])],
@@ -211,9 +218,10 @@
 
     rotate(0)
     reach(1)
+    report(2)
     rotate(1)
+    rotate(2)
     reach(2)
-    rotate(2)
     rotate(3)
     relay_sides(order[0])
     relay_col(order[1])
@@ -239,7 +247,7 @@
     for t in range(count):
         acc = jnp.zeros((wide, wide), F32)
         for at in range(0, BS, SUB):
-            left = cbuf[t, :, at : at + SUB].reshape(wide, naux)
+            left = jnp.concatenate([cbuf[t, zz, :, at : at + SUB].reshape(wide, span) for zz in range(depth)], axis=1)
             acc = acc + dot_nt(left, rbuf[t, :, at : at + SUB].reshape(wide, naux))
         acc = jnp.where(same_row, acc.reshape(groups, SUB, SUB, wide), 0.0)
         parts.append(jnp.sum(acc, axis=1).reshape(BS, wide))
@@ -284,17 +292,20 @@
             new = dot(left, tbuf[t, :, at : at + SUB].reshape(wide, naux)).astype(BF16)
             ybuf[t, :, at : at + SUB] = new.reshape(groups, SUB, SUB, naux)
 
-    gather = fold(BS, wide, lambda index: index, outer)
     parts = []
     for t in range(count):
         acc = jnp.zeros((wide, wide), F32)
         for g in range(groups):
-            acc = acc + dot_nt(cbuf[t, g].reshape(wide, naux), ybuf[t, g].reshape(wide, naux))
-        acc = jnp.where(same_sub, acc, 0.0)
-        high = acc.astype(BF16)
-        parts.append(dot(gather, high) + dot(gather, (acc - high.astype(F32)).astype(BF16)))
-    both = exact(jnp.concatenate(parts, axis=0), fold(wide, 128, outer, minor))
-    terms = [compact(both[t * BS : (t + 1) * BS]) for t in range(count)]
+            left = jnp.concatenate([cbuf[t, zz, g].reshape(wide, span) for zz in range(depth)], axis=1)
+            acc = acc + dot_nt(left, ybuf[t, g].reshape(wide, naux))
+        parts.append(jnp.where(same_sub, acc, 0.0))
+    both = exact(jnp.concatenate(parts, axis=0), fold(wide, 128, outer, minor)).reshape(count, groups, SUB, SUB, 128)
+    terms = []
+    for t in range(count):
+        total = jnp.zeros((SUB, SUB, 128), F32)
+        for g in range(groups):
+            total = jnp.where(lanes_of == g, both[t, g], total)
+        terms.append(jnp.sum(total, axis=1))
     for q in range(n_aux):
         slots = []
         for r in range(own):
@@ -350,26 +361,28 @@
     count, naux = three.shape[0], three.shape[3]
     own = occ.shape[0] // n_aux
     groups = BS // SUB
-    smem = pl.BlockSpec(memory_space=pltpu.SMEM)
     vmem = pl.BlockSpec(memory_space=pltpu.VMEM)
     hbm = pl.BlockSpec(memory_space=pl.ANY)
     tile = pltpu.VMEM((count, groups, BS, SUB, naux), BF16)
     return pl.pallas_call(
         functools.partial(fused_kernel, n_blk, n_aux, norm),
         out_shape=jax.ShapeDtypeStruct((2, own, BS * BS), F32),
-        in_specs=[smem] * 4 + [hbm, vmem, vmem, hbm],
+        in_specs=[hbm] * 8,
         out_specs=vmem,
         scratch_shapes=[
+            *(pltpu.SMEM(scalars.shape, scalars.dtype) for scalars in (sizes, rows, owners, blocks)),
+            pltpu.VMEM(occ.shape, BF16),
+            pltpu.VMEM(vir.shape, BF16),
             pltpu.VMEM((n_dev, adj.shape[0] + own, naux), BF16),
             tile,
-            tile,
+            pltpu.VMEM((count, n_blk // 2, groups, BS, SUB, naux // (n_blk // 2)), BF16),
             tile,
             tile,
             pltpu.VMEM((n_dev, own * SUB, 128), BF16),
             pltpu.VMEM((n_dev, own * SUB, 128), BF16),
             pltpu.VMEM((n_aux, own * SUB, 128), F32),
             pltpu.VMEM((n_aux, own * SUB, 128), F32),
-            pltpu.SemaphoreType.DMA,
+            pltpu.SemaphoreType.DMA((7,)),
             pltpu.SemaphoreType.DMA((count,)),
             pltpu.SemaphoreType.REGULAR((2,)),
             pltpu.SemaphoreType.DMA((4, n_blk // 2)),

time: 49.2 us -> 43.8 us (0.89)
  Pallas kernels: 46.9 us -> 41.5 us
    pallas_call x1, Pallas kernels: 46.9 us -> 41.5 us  [fused(): pl.pallas_call(functools.partial(fused_kernel, n_blk, n_aux, norm), out_s...]
where the time goes in v2:
time: 43.8 us; the launch traced here: 43.5 us
  Pallas kernels  41.5 us (95%)
  local copies, waits for them, and re-layouts  1.32 us (3%)
  between operations  0.64 us (1%)
    pallas_call x1, Pallas kernels, fused(): pl.pallas_call(functools.partial(fused_kernel, n_blk, n_aux, norm), out_s...  41.5 us
    squeeze x1, local copies, waits for them, and re-layouts, shards(): return (both[0], both[1])  1.32 us

profile of v2, /device:TPU:0, one launch (start us, length us, event | category | flops | bytes accessed | tf_op | source)
XLA Modules:
  0.0 43.5 jit_solution(9149913236776762192)
XLA Ops:
  0.6 41.5 %fused.1 = f32[2,2,1024]{2,1,0:T(2,128)} custom-call(s32[8]{0:T(128)} %sizes_hbm.1, s32[4]{0:T(128)} %rows_hbm.1, s32[4]{0:T(128)} %bitcast.7, s32[4]{0:T(128)} %blocks_hbm.1, bf16[32,1024]{1,0:T(8,128)(2,1)} %adj_hbm.1, bf16[8,1024]{1,0:T(8,128)(2,1)} %occ_hbm.1, bf16[8,1024]{1,0:T(8,128)(2,1)} %vir_hbm.1, bf16[4,32,4,8,1024]{4,3,2,1,0:T(8,128)(2,1)} %bitcast.6), custom_call_target="tpu_custom_call" | custom-call | tf_op jit(solution)/shard_map/fused/pallas_call | solution.py:367
  42.2 1.3 %slice_bitcast_fusion = (f32[2,1024]{1,0:T(2,128)}, f32[2,1024]{1,0:T(2,128)}) fusion(f32[2,2,1024]{2,1,0:T(2,128)} %fused.1), kind=kLoop, calls=%fused_computation | loop fusion | bytes 32768 | tf_op jit(solution)/shard_map/squeeze | solution.py:609

commit v3 on v2

--- a/solution.py
+++ b/solution.py
@@ -72,6 +72,7 @@
     col, sides, corner, mates = range(4)
     over_x = (b, (1 - x) * 2 + c)
     over_y = (z * 2 + 1 - y, a)
+    across = (z * 2 + 1 - y, (1 - x) * 2 + c)
     mate = (b, x * 2 + 1 - c)
     above, below = (b + 2, a), (b - 2, a)
     has_up, has_down = z < depth - 1, z > 0
@@ -85,7 +86,7 @@
     def tell(sem, device):
         pl.semaphore_signal(sem, inc=1, device_id=device, device_id_type=MESH)
 
-    for device in (over_x, over_y, mate):
+    for device in (over_x, over_y, across, mate):
         tell(barrier, device)
     pl.when(has_up)(lambda: tell(barrier, above))
     pl.when(has_down)(lambda: tell(barrier, below))
@@ -116,7 +117,7 @@
     mine = [jnp.where(live(sizes[a * own + r]), pick(vir_all, a * own + r), 0.0) for r in range(own)]
     got[me, arows:, :] = jnp.concatenate(mine, axis=0).astype(BF16)
 
-    pl.semaphore_wait(barrier, 3 + has_up.astype(jnp.int32) + has_down.astype(jnp.int32))
+    pl.semaphore_wait(barrier, 4 + has_up.astype(jnp.int32) + has_down.astype(jnp.int32))
 
     def send(block, device, kind, zz, part=None):
         ref = got.at[block] if part is None else got.at[block, part]
@@ -137,6 +138,7 @@
         send(me, device, sides, z)
     pl.when(has_up)(lambda: send(me, above, col, z))
     pl.when(has_down)(lambda: send(me, below, col, z))
+    send(me, across, corner, z)
     send(me, mate, mates, z)
 
     def report(hop):
@@ -161,17 +163,21 @@
         send(block, over_y, sides, zz)
         send(block, mate, mates, zz)
 
-    def relay_sides(zz):
+    def relay_sides(zz, halves=True):
         arrive(sides, zz, 2)
         block_x, block_y = ident(1 - x, y, zz, c), ident(x, 1 - y, zz, c)
-        send(block_x, over_y, corner, zz, pl.ds(0, half))
-        send(block_y, over_x, corner, zz, pl.ds(half, arows + own - half))
+        if halves:
+            send(block_x, over_y, corner, zz, pl.ds(0, half))
+            send(block_y, over_x, corner, zz, pl.ds(half, arows + own - half))
         send(block_x, mate, mates, zz)
         send(block_y, mate, mates, zz)
 
     def relay_corner(zz):
         arrive(corner, zz, 1)
         send(ident(1 - x, 1 - y, zz, c), mate, mates, zz)
+
+    def ready(zz):
+        arrive(mates, zz, 4)
 
     low = z < depth // 2
     zl = jnp.where(low, z, depth - 1 - z)
@@ -202,37 +208,38 @@
     def contract(k, t):
         zz = order[k]
         part = got[pl.ds(zz * per_plane, per_plane), :arows, :].reshape(span, naux)
-        new = dot_nt(tbuf[t].reshape(pairs, naux), part).astype(BF16)
-        cbuf[t, zz] = new.reshape(groups, BS, SUB, span)
-
-    events = {
-        (0, 1): [lambda: relay_sides(order[1])],
-        (0, 3): [lambda: relay_col(order[3])],
-        (1, 0): [lambda: relay_sides(order[2]), lambda: relay_corner(order[1]), lambda: arrive(mates, order[1], 4)],
-        (1, 1): [lambda: relay_corner(order[2])],
-        (1, 3): [lambda: relay_sides(order[3])],
-        (2, 0): [lambda: arrive(mates, order[2], 4)],
-        (2, 2): [lambda: relay_corner(order[3])],
-        (3, 0): [lambda: arrive(mates, order[3], 4)],
-    }
-
-    rotate(0)
+        for first in range(0, groups, groups // 2):
+            rows_of = pl.ds(first, groups // 2)
+            new = dot_nt(tbuf[t, rows_of].reshape(pairs // 2, naux), part).astype(BF16)
+            cbuf[t, zz, rows_of] = new.reshape(groups // 2, BS, SUB, span)
+
     reach(1)
     report(2)
+    rotate(0)
+    reach(2)
     rotate(1)
+    relay_sides(z, halves=False)
+    relay_col(order[1])
     rotate(2)
-    reach(2)
     rotate(3)
-    relay_sides(order[0])
-    relay_col(order[1])
-    relay_corner(order[0])
+    relay_corner(z)
     relay_col(order[2])
-    arrive(mates, order[0], 4)
+    relay_sides(order[1])
+    arrive(mates, z, 4)
+    events = {
+        (0, 1): [(relay_col, 3)],
+        (1, 0): [(relay_corner, 1), (relay_sides, 2), (ready, 1)],
+        (1, 1): [(relay_corner, 2), (relay_sides, 3)],
+        (2, 0): [(ready, 2)],
+        (2, 1): [(relay_corner, 3)],
+        (3, 0): [(ready, 3)],
+    }
     for k in range(depth):
-        for t in range(count):
-            for event in events.get((k, t), []):
-                event()
-            contract(k, t)
+        for part in range(2):
+            for event, which in events.get((k, part), []):
+                event(order[which])
+            for t in range(part * count // 2, (part + 1) * count // 2):
+                contract(k, t)
 
     same_row = iota((SUB, SUB, wide), 0) == iota((SUB, SUB, wide), 2) % (SUB * SUB) // SUB
     lanes_of = iota((SUB, 128), 1) // BS

time: 43.8 us -> 42.2 us (0.963)
  Pallas kernels: 41.5 us -> 39.9 us
    pallas_call x1, Pallas kernels: 41.5 us -> 39.9 us  [fused(): pl.pallas_call(functools.partial(fused_kernel, n_blk, n_aux, norm), out_s...]
where the time goes in v3:
time: 42.2 us; the launch traced here: 41.9 us
  Pallas kernels  39.9 us (95%)
  local copies, waits for them, and re-layouts  1.32 us (3%)
  between operations  0.64 us (2%)
    pallas_call x1, Pallas kernels, fused(): pl.pallas_call(functools.partial(fused_kernel, n_blk, n_aux, norm), out_s...  39.9 us
    squeeze x1, local copies, waits for them, and re-layouts, shards(): return (both[0], both[1])  1.32 us

profile of v3, /device:TPU:0, one launch (start us, length us, event | category | flops | bytes accessed | tf_op | source)
XLA Modules:
  0.0 41.9 jit_solution(17425486788836295460)
XLA Ops:
  0.6 39.9 %fused.1 = f32[2,2,1024]{2,1,0:T(2,128)} custom-call(s32[8]{0:T(128)} %sizes_hbm.1, s32[4]{0:T(128)} %rows_hbm.1, s32[4]{0:T(128)} %bitcast.7, s32[4]{0:T(128)} %blocks_hbm.1, bf16[32,1024]{1,0:T(8,128)(2,1)} %adj_hbm.1, bf16[8,1024]{1,0:T(8,128)(2,1)} %occ_hbm.1, bf16[8,1024]{1,0:T(8,128)(2,1)} %vir_hbm.1, bf16[4,32,4,8,1024]{4,3,2,1,0:T(8,128)(2,1)} %bitcast.6), custom_call_target="tpu_custom_call" | custom-call | tf_op jit(solution)/shard_map/fused/pallas_call | solution.py:374
  40.6 1.3 %slice_bitcast_fusion = (f32[2,1024]{1,0:T(2,128)}, f32[2,1024]{1,0:T(2,128)}) fusion(f32[2,2,1024]{2,1,0:T(2,128)} %fused.1), kind=kLoop, calls=%fused_computation | loop fusion | bytes 32768 | tf_op jit(solution)/shard_map/squeeze | solution.py:616

commit v4 on v3

--- a/solution.py
+++ b/solution.py
@@ -53,7 +53,7 @@
     n_blk, n_aux, norm,
     sizes_hbm, rows_hbm, owners_hbm, blocks_hbm, adj_hbm, occ_hbm, vir_hbm, t_hbm,
     out_ref,
-    sizes, rows, owners, blocks, occ_ref, vir_ref, got, tbuf, cbuf, rbuf, ybuf, vir_send, vir_got, occ_send, occ_got,
+    sizes, rows, owners, blocks, occ_ref, vir_ref, got, tbuf, cbuf, rbuf, ybuf, vir_acc, vir_send, vir_got, occ_send, occ_got,
     in_sem, t_sem, near_sem, recv_sem, send_sem, trade_sem,
 ):
     n_dev = n_blk * n_aux
@@ -63,7 +63,6 @@
     wide = BS * SUB
     own = out_ref.shape[1]
     arows = adj_hbm.shape[0]
-    half = arows // 2
     span = naux // depth
     per_plane = n_dev // depth
     b = lax.axis_index("blk")
@@ -76,6 +75,7 @@
     mate = (b, x * 2 + 1 - c)
     above, below = (b + 2, a), (b - 2, a)
     has_up, has_down = z < depth - 1, z > 0
+    inner_plane = has_up & has_down
     me = b * n_aux + a
 
     def ident(xx, yy, zz, cc):
@@ -134,8 +134,12 @@
         part = got.at[pl.ds(0, number)]
         pltpu.make_async_copy(part, part, recv_sem.at[kind, zz]).wait()
 
-    for device in (over_x, over_y):
-        send(me, device, sides, z)
+    def turn(even, odd):
+        return tuple(jnp.where(c == 0, i, j) for i, j in zip(even, odd))
+
+    near_one, near_two = turn(over_x, over_y), turn(over_y, over_x)
+    send(me, near_one, sides, z)
+    send(me, near_two, sides, z)
     pl.when(has_up)(lambda: send(me, above, col, z))
     pl.when(has_down)(lambda: send(me, below, col, z))
     send(me, across, corner, z)
@@ -146,35 +150,34 @@
         pl.when(has_up & (z - hop >= 0))(lambda: tell(near_sem.at[1], above))
 
     def reach(hop):
-        @pl.when(z + hop + 1 < depth)
-        def _():
-            pl.semaphore_wait(near_sem.at[0], 1)
-            send(me, (b + 2 * (hop + 1), a), col, z)
-
-        @pl.when(z - hop - 1 >= 0)
-        def _():
-            pl.semaphore_wait(near_sem.at[1], 1)
-            send(me, (b - 2 * (hop + 1), a), col, z)
+        pl.when(z + hop + 1 < depth)(lambda: pl.semaphore_wait(near_sem.at[0], 1))
+        pl.when(z - hop - 1 >= 0)(lambda: pl.semaphore_wait(near_sem.at[1], 1))
+
+    def send_far(hop):
+        pl.when(z + hop < depth)(lambda: send(me, (b + 2 * hop, a), col, z))
+        pl.when(z - hop >= 0)(lambda: send(me, (b - 2 * hop, a), col, z))
 
     def relay_col(zz):
         block = ident(x, y, zz, c)
         arrive(col, zz, 1)
-        send(block, over_x, sides, zz)
-        send(block, over_y, sides, zz)
+        pl.when((zz == z - 1) & has_up)(lambda: send(block, above, col, zz))
+        pl.when((zz == z + 1) & has_down)(lambda: send(block, below, col, zz))
+        send(block, near_one, sides, zz)
+        send(block, near_two, sides, zz)
+        send(block, across, corner, zz)
         send(block, mate, mates, zz)
 
-    def relay_sides(zz, halves=True):
+    def relay_sides(zz):
         arrive(sides, zz, 2)
-        block_x, block_y = ident(1 - x, y, zz, c), ident(x, 1 - y, zz, c)
-        if halves:
-            send(block_x, over_y, corner, zz, pl.ds(0, half))
-            send(block_y, over_x, corner, zz, pl.ds(half, arows + own - half))
-        send(block_x, mate, mates, zz)
-        send(block_y, mate, mates, zz)
+        send(ident(1 - x, y, zz, c), mate, mates, zz)
+        send(ident(x, 1 - y, zz, c), mate, mates, zz)
 
     def relay_corner(zz):
         arrive(corner, zz, 1)
         send(ident(1 - x, 1 - y, zz, c), mate, mates, zz)
+
+    def relay_outer(zz):
+        pl.when(jnp.logical_not(inner_plane))(lambda: relay_col(zz))
 
     def ready(zz):
         arrive(mates, zz, 4)
@@ -203,7 +206,9 @@
         left = jnp.where(same_sub, spread, 0.0).astype(BF16)
         pltpu.make_async_copy(tbuf.at[t], tbuf.at[t], t_sem.at[t]).wait()
         for g in range(groups):
-            rbuf[t, g] = dot(left, tbuf[t, g].reshape(wide, naux)).astype(BF16).reshape(BS, SUB, naux)
+            new = dot(left, tbuf[t, g].reshape(wide, naux)).astype(BF16)
+            for zz in range(depth):
+                rbuf[t, zz, g] = new[:, zz * span : (zz + 1) * span].reshape(BS, SUB, span)
 
     def contract(k, t):
         zz = order[k]
@@ -213,33 +218,45 @@
             new = dot_nt(tbuf[t, rows_of].reshape(pairs // 2, naux), part).astype(BF16)
             cbuf[t, zz, rows_of] = new.reshape(groups // 2, BS, SUB, span)
 
+    def column_term(k, t):
+        zz = order[k]
+        acc = jnp.zeros((wide, wide), F32) if k == 0 else vir_acc[t]
+        for at in range(0, BS, SUB):
+            left = cbuf[t, zz, :, at : at + SUB].reshape(wide, span)
+            acc = acc + dot_nt(left, rbuf[t, zz, :, at : at + SUB].reshape(wide, span))
+        return acc
+
     reach(1)
     report(2)
     rotate(0)
     reach(2)
     rotate(1)
-    relay_sides(z, halves=False)
     relay_col(order[1])
+    pl.when(inner_plane)(lambda: relay_col(order[2]))
     rotate(2)
+    relay_sides(z)
     rotate(3)
+    send_far(3)
     relay_corner(z)
-    relay_col(order[2])
-    relay_sides(order[1])
-    arrive(mates, z, 4)
+    ready(z)
     events = {
-        (0, 1): [(relay_col, 3)],
-        (1, 0): [(relay_corner, 1), (relay_sides, 2), (ready, 1)],
-        (1, 1): [(relay_corner, 2), (relay_sides, 3)],
+        (0, 1): [(relay_sides, 1), (relay_outer, 2), (relay_corner, 1)],
+        (1, 0): [(relay_col, 3), (ready, 1)],
+        (1, 1): [(relay_sides, 2), (relay_corner, 2)],
         (2, 0): [(ready, 2)],
-        (2, 1): [(relay_corner, 3)],
+        (2, 1): [(relay_sides, 3), (relay_corner, 3)],
         (3, 0): [(ready, 3)],
     }
     for k in range(depth):
         for part in range(2):
             for event, which in events.get((k, part), []):
                 event(order[which])
-            for t in range(part * count // 2, (part + 1) * count // 2):
+            tiles_here = range(part * count // 2, (part + 1) * count // 2)
+            for t in tiles_here:
                 contract(k, t)
+            if k < depth - 1:
+                for t in tiles_here:
+                    vir_acc[t] = column_term(k, t)
 
     same_row = iota((SUB, SUB, wide), 0) == iota((SUB, SUB, wide), 2) % (SUB * SUB) // SUB
     lanes_of = iota((SUB, 128), 1) // BS
@@ -252,10 +269,7 @@
 
     parts = []
     for t in range(count):
-        acc = jnp.zeros((wide, wide), F32)
-        for at in range(0, BS, SUB):
-            left = jnp.concatenate([cbuf[t, zz, :, at : at + SUB].reshape(wide, span) for zz in range(depth)], axis=1)
-            acc = acc + dot_nt(left, rbuf[t, :, at : at + SUB].reshape(wide, naux))
+        acc = column_term(depth - 1, t)
         acc = jnp.where(same_row, acc.reshape(groups, SUB, SUB, wide), 0.0)
         parts.append(jnp.sum(acc, axis=1).reshape(BS, wide))
     both = exact(jnp.concatenate(parts, axis=0), fold(wide, 128, inner, minor))
@@ -360,7 +374,8 @@
 
     done(vir_send.at[pl.ds(0, n_dev - 1)], trade_sem.at[0])
     done(occ_send.at[pl.ds(0, n_aux - 1)], trade_sem.at[2])
-    done(got.at[pl.ds(0, depth - 1 + 7 * depth)], send_sem)
+    pl.when(inner_plane)(lambda: done(got.at[pl.ds(0, 7 * depth + 4)], send_sem))
+    pl.when(jnp.logical_not(inner_plane))(lambda: done(got.at[pl.ds(0, 7 * depth + 2)], send_sem))
 
 
 def fused(sizes, rows, owners, blocks, adj, occ, vir, three, n_blk, n_aux, norm):
@@ -371,6 +386,7 @@
     vmem = pl.BlockSpec(memory_space=pltpu.VMEM)
     hbm = pl.BlockSpec(memory_space=pl.ANY)
     tile = pltpu.VMEM((count, groups, BS, SUB, naux), BF16)
+    by_plane = pltpu.VMEM((count, n_blk // 2, groups, BS, SUB, naux // (n_blk // 2)), BF16)
     return pl.pallas_call(
         functools.partial(fused_kernel, n_blk, n_aux, norm),
         out_shape=jax.ShapeDtypeStruct((2, own, BS * BS), F32),
@@ -382,9 +398,10 @@
             pltpu.VMEM(vir.shape, BF16),
             pltpu.VMEM((n_dev, adj.shape[0] + own, naux), BF16),
             tile,
-            pltpu.VMEM((count, n_blk // 2, groups, BS, SUB, naux // (n_blk // 2)), BF16),
+            by_plane,
+            by_plane,
             tile,
-            tile,
+            pltpu.VMEM((count, BS * SUB, BS * SUB), F32),
             pltpu.VMEM((n_dev, own * SUB, 128), BF16),
             pltpu.VMEM((n_dev, own * SUB, 128), BF16),
             pltpu.VMEM((n_aux, own * SUB, 128), F32),

time: 42.2 us -> 37.8 us (0.90)
  Pallas kernels: 39.9 us -> 35.5 us
    pallas_call x1, Pallas kernels: 39.9 us -> 35.5 us  [fused(): pl.pallas_call(functools.partial(fused_kernel, n_blk, n_aux, norm), out_s...]
where the time goes in v4:
time: 37.8 us; the launch traced here: 37.5 us
  Pallas kernels  35.5 us (94%)
  local copies, waits for them, and re-layouts  1.32 us (3%)
  between operations  0.64 us (2%)
    pallas_call x1, Pallas kernels, fused(): pl.pallas_call(functools.partial(fused_kernel, n_blk, n_aux, norm), out_s...  35.5 us
    squeeze x1, local copies, waits for them, and re-layouts, shards(): return (both[0], both[1])  1.32 us

profile of v4, /device:TPU:0, one launch (start us, length us, event | category | flops | bytes accessed | tf_op | source)
XLA Modules:
  0.0 37.5 jit_solution(7526782511519445195)
XLA Ops:
  0.6 35.5 %fused.1 = f32[2,2,1024]{2,1,0:T(2,128)} custom-call(s32[8]{0:T(128)} %sizes_hbm.1, s32[4]{0:T(128)} %rows_hbm.1, s32[4]{0:T(128)} %bitcast.7, s32[4]{0:T(128)} %blocks_hbm.1, bf16[32,1024]{1,0:T(8,128)(2,1)} %adj_hbm.1, bf16[8,1024]{1,0:T(8,128)(2,1)} %occ_hbm.1, bf16[8,1024]{1,0:T(8,128)(2,1)} %vir_hbm.1, bf16[4,32,4,8,1024]{4,3,2,1,0:T(8,128)(2,1)} %bitcast.6), custom_call_target="tpu_custom_call" | custom-call | tf_op jit(solution)/shard_map/fused/pallas_call | solution.py:390
  36.2 1.3 %slice_bitcast_fusion = (f32[2,1024]{1,0:T(2,128)}, f32[2,1024]{1,0:T(2,128)}) fusion(f32[2,2,1024]{2,1,0:T(2,128)} %fused.1), kind=kLoop, calls=%fused_computation | loop fusion | bytes 32768 | tf_op jit(solution)/shard_map/squeeze | solution.py:633

commit v5 on v4

--- a/solution.py
+++ b/solution.py
@@ -119,8 +119,8 @@
 
     pl.semaphore_wait(barrier, 4 + has_up.astype(jnp.int32) + has_down.astype(jnp.int32))
 
-    def send(block, device, kind, zz, part=None):
-        ref = got.at[block] if part is None else got.at[block, part]
+    def send(block, device, kind, zz):
+        ref = got.at[block]
         pltpu.make_async_remote_copy(
             src_ref=ref,
             dst_ref=ref,
@@ -138,11 +138,11 @@
         return tuple(jnp.where(c == 0, i, j) for i, j in zip(even, odd))
 
     near_one, near_two = turn(over_x, over_y), turn(over_y, over_x)
+    send(me, across, corner, z)
     send(me, near_one, sides, z)
     send(me, near_two, sides, z)
     pl.when(has_up)(lambda: send(me, above, col, z))
     pl.when(has_down)(lambda: send(me, below, col, z))
-    send(me, across, corner, z)
     send(me, mate, mates, z)
 
     def report(hop):
@@ -162,9 +162,9 @@
         arrive(col, zz, 1)
         pl.when((zz == z - 1) & has_up)(lambda: send(block, above, col, zz))
         pl.when((zz == z + 1) & has_down)(lambda: send(block, below, col, zz))
+        send(block, across, corner, zz)
         send(block, near_one, sides, zz)
         send(block, near_two, sides, zz)
-        send(block, across, corner, zz)
         send(block, mate, mates, zz)
 
     def relay_sides(zz):
@@ -233,10 +233,10 @@
     rotate(1)
     relay_col(order[1])
     pl.when(inner_plane)(lambda: relay_col(order[2]))
+    send_far(3)
     rotate(2)
     relay_sides(z)
     rotate(3)
-    send_far(3)
     relay_corner(z)
     ready(z)
     events = {
@@ -285,7 +285,7 @@
         vir_send[p] = jnp.concatenate(slots, axis=0).astype(BF16)
     vir_got[me] = vir_send[me]
 
-    def send_vir(k, carry):
+    def send_vir(k):
         p = lax.rem(me + k, n_dev)
         pltpu.make_async_remote_copy(
             src_ref=vir_send.at[p],
@@ -295,9 +295,6 @@
             device_id=(p // n_aux, p % n_aux),
             device_id_type=MESH,
         ).start()
-        return carry
-
-    lax.fori_loop(1, n_dev, send_vir, 0)
 
     parts = []
     for t in range(count):
@@ -309,6 +306,8 @@
         spread = square_v[t * BS : (t + 1) * BS].reshape(groups, 1, SUB, wide)
         spread = jnp.broadcast_to(spread, (groups, SUB, SUB, wide))
         left = jnp.where(same_row, spread, 0.0).reshape(wide, wide).astype(BF16)
+        for k in range(max(1, t * n_dev // count), (t + 1) * n_dev // count):
+            send_vir(k)
         for at in range(0, BS, SUB):
             new = dot(left, tbuf[t, :, at : at + SUB].reshape(wide, naux)).astype(BF16)
             ybuf[t, :, at : at + SUB] = new.reshape(groups, SUB, SUB, naux)
@@ -384,12 +383,12 @@
     own = occ.shape[0] // n_aux
     groups = BS // SUB
     vmem = pl.BlockSpec(memory_space=pltpu.VMEM)
-    hbm = pl.BlockSpec(memory_space=pl.ANY)
+    hbm = pl.BlockSpec(memory_space=pltpu.HBM)
     tile = pltpu.VMEM((count, groups, BS, SUB, naux), BF16)
     by_plane = pltpu.VMEM((count, n_blk // 2, groups, BS, SUB, naux // (n_blk // 2)), BF16)
     return pl.pallas_call(
         functools.partial(fused_kernel, n_blk, n_aux, norm),
-        out_shape=jax.ShapeDtypeStruct((2, own, BS * BS), F32),
+        out_shape=pltpu.VMEM((2, own, BS * BS), F32),
         in_specs=[hbm] * 8,
         out_specs=vmem,
         scratch_shapes=[
@@ -414,7 +413,7 @@
             pltpu.SemaphoreType.DMA((4,)),
         ],
         compiler_params=pltpu.CompilerParams(
-            collective_id=0, has_side_effects=True, vmem_limit_bytes=67043328
+            collective_id=0, has_side_effects=True, vmem_limit_bytes=60 << 20
         ),
         name="fused",
     )(sizes, rows, owners, blocks, adj, occ, vir, three.reshape(count, BS, groups, SUB, naux))

time: 37.8 us -> 36.9 us (0.976)
  local copies, waits for them, and re-layouts: 1.32 us -> 0.61 us
    squeeze x1, local copies, waits for them, and re-layouts: 1.32 us -> 0.61 us  [shards(): return (both[0], both[1])]
where the time goes in v5:
time: 36.9 us; the launch traced here: 36.7 us
  Pallas kernels  35.4 us (96%)
  between operations  0.64 us (2%)
  local copies, waits for them, and re-layouts  0.61 us (2%)
    pallas_call x1, Pallas kernels, fused(): pl.pallas_call(functools.partial(fused_kernel, n_blk, n_aux, norm), out_s...  35.4 us

profile of v5, /device:TPU:0, one launch (start us, length us, event | category | flops | bytes accessed | tf_op | source)
XLA Modules:
  0.0 36.7 jit_solution(17598692384382263275)
XLA Ops:
  0.6 35.4 %fused.1 = f32[2,2,1024]{2,1,0:T(2,128)S(1)} custom-call(s32[8]{0:T(128)} %sizes_hbm.1, s32[4]{0:T(128)} %rows_hbm.1, s32[4]{0:T(128)} %bitcast.7, s32[4]{0:T(128)} %blocks_hbm.1, bf16[32,1024]{1,0:T(8,128)(2,1)} %adj_hbm.1, bf16[8,1024]{1,0:T(8,128)(2,1)} %occ_hbm.1, bf16[8,1024]{1,0:T(8,128)(2,1)} %vir_hbm.1, bf16[4,32,4,8,1024]{4,3,2,1,0:T(8,128)(2,1)} %bitcast.6), custom_call_target="tpu_custom_call" | custom-call | tf_op jit(solution)/shard_map/fused/pallas_call | solution.py:389
  36.1 0.6 %slice_bitcast_fusion = (f32[2,1024]{1,0:T(2,128)}, f32[2,1024]{1,0:T(2,128)}) fusion(f32[2,2,1024]{2,1,0:T(2,128)S(1)} %fused.1), kind=kLoop, calls=%fused_computation | loop fusion | bytes 32768 | tf_op jit(solution)/shard_map/squeeze | solution.py:632

commit v6 on v5

--- a/solution.py
+++ b/solution.py
@@ -53,8 +53,8 @@
     n_blk, n_aux, norm,
     sizes_hbm, rows_hbm, owners_hbm, blocks_hbm, adj_hbm, occ_hbm, vir_hbm, t_hbm,
     out_ref,
-    sizes, rows, owners, blocks, occ_ref, vir_ref, got, tbuf, cbuf, rbuf, ybuf, vir_acc, vir_send, vir_got, occ_send, occ_got,
-    in_sem, t_sem, near_sem, recv_sem, send_sem, trade_sem,
+    sizes, rows, owners, blocks, occ_ref, vir_ref, got, vgot, tbuf, cbuf, rbuf, ybuf, vir_acc, vir_send, vir_got, occ_send, occ_got,
+    in_sem, t_sem, near_sem, recv_sem, send_sem, v_sem, trade_sem,
 ):
     n_dev = n_blk * n_aux
     depth = n_blk // 2
@@ -81,6 +81,9 @@
     def ident(xx, yy, zz, cc):
         return ((zz * 2 + yy) * 2 + xx) * 2 + cc
 
+    def stand(xx, yy, cc):
+        return (yy * 2 + xx) * 2 + cc
+
     barrier = pltpu.get_barrier_semaphore()
 
     def tell(sem, device):
@@ -92,7 +95,7 @@
     pl.when(has_down)(lambda: tell(barrier, below))
 
     pairs_in = (
-        (vir_hbm, vir_ref), (sizes_hbm, sizes), (adj_hbm, got.at[me, pl.ds(0, arows)]),
+        (vir_hbm, vir_ref), (sizes_hbm, sizes), (adj_hbm, got.at[me]),
         (rows_hbm, rows), (occ_hbm, occ_ref), (owners_hbm, owners), (blocks_hbm, blocks),
     )
     fetches = [pltpu.make_async_copy(src, dst, in_sem.at[i]) for i, (src, dst) in enumerate(pairs_in)]
@@ -115,7 +118,7 @@
             pltpu.make_async_copy(t_hbm.at[t, :, g], tbuf.at[t, g], t_sem.at[t]).start()
     vir_all = vir_ref[...].astype(F32)
     mine = [jnp.where(live(sizes[a * own + r]), pick(vir_all, a * own + r), 0.0) for r in range(own)]
-    got[me, arows:, :] = jnp.concatenate(mine, axis=0).astype(BF16)
+    vgot[stand(x, y, c), z] = jnp.concatenate(mine, axis=0).astype(BF16)
 
     pl.semaphore_wait(barrier, 4 + has_up.astype(jnp.int32) + has_down.astype(jnp.int32))
 
@@ -134,10 +137,43 @@
         part = got.at[pl.ds(0, number)]
         pltpu.make_async_copy(part, part, recv_sem.at[kind, zz]).wait()
 
+    v_col, v_sides, v_mates, v_sent_col, v_sent = range(5)
+
+    def send_v(ref, device, kind):
+        pltpu.make_async_remote_copy(
+            src_ref=ref,
+            dst_ref=ref,
+            send_sem=v_sem.at[v_sent_col if kind == v_col else v_sent],
+            recv_sem=v_sem.at[kind],
+            device_id=device,
+            device_id_type=MESH,
+        ).start()
+
+    def spread_v(hop):
+        mine_v = vgot.at[stand(x, y, c), z]
+        pl.when(z + hop < depth)(lambda: send_v(mine_v, (b + 2 * hop, a), v_col))
+        pl.when(z - hop >= 0)(lambda: send_v(mine_v, (b - 2 * hop, a), v_col))
+
+    def wait_v(ref, kind):
+        pltpu.make_async_copy(ref, ref, v_sem.at[kind]).wait()
+
+    def relay_v_col():
+        wait_v(vgot.at[0, pl.ds(0, depth - 1)], v_col)
+        column = vgot.at[stand(x, y, c)]
+        for device in (across, near_one, near_two):
+            send_v(column, device, v_sides)
+        send_v(column, mate, v_mates)
+
+    def relay_v_sides():
+        wait_v(vgot.at[pl.ds(0, 3)], v_sides)
+        for xx, yy in ((1 - x, y), (x, 1 - y), (1 - x, 1 - y)):
+            send_v(vgot.at[stand(xx, yy, c)], mate, v_mates)
+
     def turn(even, odd):
         return tuple(jnp.where(c == 0, i, j) for i, j in zip(even, odd))
 
     near_one, near_two = turn(over_x, over_y), turn(over_y, over_x)
+    spread_v(1)
     send(me, across, corner, z)
     send(me, near_one, sides, z)
     send(me, near_two, sides, z)
@@ -212,7 +248,7 @@
 
     def contract(k, t):
         zz = order[k]
-        part = got[pl.ds(zz * per_plane, per_plane), :arows, :].reshape(span, naux)
+        part = got[pl.ds(zz * per_plane, per_plane)].reshape(span, naux)
         for first in range(0, groups, groups // 2):
             rows_of = pl.ds(first, groups // 2)
             new = dot_nt(tbuf[t, rows_of].reshape(pairs // 2, naux), part).astype(BF16)
@@ -228,22 +264,48 @@
 
     reach(1)
     report(2)
+    spread_v(2)
     rotate(0)
     reach(2)
+    spread_v(3)
     rotate(1)
     relay_col(order[1])
     pl.when(inner_plane)(lambda: relay_col(order[2]))
+    rotate(2)
+    rotate(3)
     send_far(3)
-    rotate(2)
     relay_sides(z)
-    rotate(3)
     relay_corner(z)
     ready(z)
+    same_row = iota((SUB, SUB, wide), 0) == iota((SUB, SUB, wide), 2) % (SUB * SUB) // SUB
+    square_v = []
+
+    def prepare():
+        wait_v(vgot.at[pl.ds(0, 4)], v_mates)
+        parts = []
+        for t in range(count):
+            slot = blocks[t] // own
+            near = vgot[stand(slot // 2, owners[t] % 2, slot % 2), owners[t] // 2]
+            parts.append(jnp.where(diag, pick(near.astype(F32), blocks[t] % own), 0.0))
+        square_v.append(dot(jnp.concatenate(parts, axis=0).astype(BF16), fold(pairs, wide, minor, inner)))
+
+    def expand(tiles_here):
+        for t in tiles_here:
+            spread = square_v[0][t * BS : (t + 1) * BS].reshape(groups, 1, SUB, wide)
+            spread = jnp.broadcast_to(spread, (groups, SUB, SUB, wide))
+            left = jnp.where(same_row, spread, 0.0).reshape(wide, wide).astype(BF16)
+            for at in range(0, BS, SUB):
+                new = dot(left, tbuf[t, :, at : at + SUB].reshape(wide, naux)).astype(BF16)
+                ybuf[t, :, at : at + SUB] = new.reshape(groups, SUB, SUB, naux)
+
     events = {
-        (0, 1): [(relay_sides, 1), (relay_outer, 2), (relay_corner, 1)],
+        (0, 1): [(lambda zz: relay_v_col(), 1), (relay_sides, 1), (relay_outer, 2), (relay_corner, 1)],
         (1, 0): [(relay_col, 3), (ready, 1)],
-        (1, 1): [(relay_sides, 2), (relay_corner, 2)],
-        (2, 0): [(ready, 2)],
+        (1, 1): [(lambda zz: relay_v_sides(), 2)],
+        (2, 0): [
+            (lambda zz: prepare(), 2), (lambda zz: expand((0, 1)), 2), (relay_sides, 2), (relay_corner, 2),
+            (lambda zz: expand((2, 3)), 2), (ready, 2),
+        ],
         (2, 1): [(relay_sides, 3), (relay_corner, 3)],
         (3, 0): [(ready, 3)],
     }
@@ -254,11 +316,9 @@
             tiles_here = range(part * count // 2, (part + 1) * count // 2)
             for t in tiles_here:
                 contract(k, t)
-            if k < depth - 1:
-                for t in tiles_here:
-                    vir_acc[t] = column_term(k, t)
-
-    same_row = iota((SUB, SUB, wide), 0) == iota((SUB, SUB, wide), 2) % (SUB * SUB) // SUB
+            for t in tiles_here:
+                vir_acc[t] = column_term(k, t)
+
     lanes_of = iota((SUB, 128), 1) // BS
 
     def compact(square):
@@ -269,8 +329,7 @@
 
     parts = []
     for t in range(count):
-        acc = column_term(depth - 1, t)
-        acc = jnp.where(same_row, acc.reshape(groups, SUB, SUB, wide), 0.0)
+        acc = jnp.where(same_row, vir_acc[t].reshape(groups, SUB, SUB, wide), 0.0)
         parts.append(jnp.sum(acc, axis=1).reshape(BS, wide))
     both = exact(jnp.concatenate(parts, axis=0), fold(wide, 128, inner, minor))
     terms = [compact(both[t * BS : (t + 1) * BS]) for t in range(count)]
@@ -285,8 +344,7 @@
         vir_send[p] = jnp.concatenate(slots, axis=0).astype(BF16)
     vir_got[me] = vir_send[me]
 
-    def send_vir(k):
-        p = lax.rem(me + k, n_dev)
+    def send_vir(p):
         pltpu.make_async_remote_copy(
             src_ref=vir_send.at[p],
             dst_ref=vir_got.at[me],
@@ -298,22 +356,10 @@
 
     parts = []
     for t in range(count):
-        home = owners[t] * n_aux + blocks[t] // own
-        row = pick(got[home, arows:, :].astype(F32), blocks[t] % own)
-        parts.append(jnp.where(diag, row, 0.0))
-    square_v = dot(jnp.concatenate(parts, axis=0).astype(BF16), fold(pairs, wide, minor, inner))
-    for t in range(count):
-        spread = square_v[t * BS : (t + 1) * BS].reshape(groups, 1, SUB, wide)
-        spread = jnp.broadcast_to(spread, (groups, SUB, SUB, wide))
-        left = jnp.where(same_row, spread, 0.0).reshape(wide, wide).astype(BF16)
-        for k in range(max(1, t * n_dev // count), (t + 1) * n_dev // count):
-            send_vir(k)
-        for at in range(0, BS, SUB):
-            new = dot(left, tbuf[t, :, at : at + SUB].reshape(wide, naux)).astype(BF16)
-            ybuf[t, :, at : at + SUB] = new.reshape(groups, SUB, SUB, naux)
-
-    parts = []
-    for t in range(count):
+        if t == 0:
+            for k in reversed(range(depth)):
+                for i in range(0 if k else 1, per_plane):
+                    send_vir(order[k] * per_plane + lax.rem(me + i, per_plane))
         acc = jnp.zeros((wide, wide), F32)
         for g in range(groups):
             left = jnp.concatenate([cbuf[t, zz, g].reshape(wide, span) for zz in range(depth)], axis=1)
@@ -373,6 +419,8 @@
 
     done(vir_send.at[pl.ds(0, n_dev - 1)], trade_sem.at[0])
     done(occ_send.at[pl.ds(0, n_aux - 1)], trade_sem.at[2])
+    done(vgot.at[0, pl.ds(0, depth - 1)], v_sem.at[v_sent_col])
+    done(vgot.at[pl.ds(0, 7)], v_sem.at[v_sent])
     pl.when(inner_plane)(lambda: done(got.at[pl.ds(0, 7 * depth + 4)], send_sem))
     pl.when(jnp.logical_not(inner_plane))(lambda: done(got.at[pl.ds(0, 7 * depth + 2)], send_sem))
 
@@ -395,7 +443,8 @@
             *(pltpu.SMEM(scalars.shape, scalars.dtype) for scalars in (sizes, rows, owners, blocks)),
             pltpu.VMEM(occ.shape, BF16),
             pltpu.VMEM(vir.shape, BF16),
-            pltpu.VMEM((n_dev, adj.shape[0] + own, naux), BF16),
+            pltpu.VMEM((n_dev, adj.shape[0], naux), BF16),
+            pltpu.VMEM((2 * n_aux, n_blk // 2, own, naux), BF16),
             tile,
             by_plane,
             by_plane,
@@ -410,6 +459,7 @@
             pltpu.SemaphoreType.REGULAR((2,)),
             pltpu.SemaphoreType.DMA((4, n_blk // 2)),
             pltpu.SemaphoreType.DMA,
+            pltpu.SemaphoreType.DMA((5,)),
             pltpu.SemaphoreType.DMA((4,)),
         ],
         compiler_params=pltpu.CompilerParams(

time: 36.9 us -> 34.9 us (0.946)
  Pallas kernels: 35.4 us -> 33.4 us
    pallas_call x1, Pallas kernels: 35.4 us -> 33.4 us  [fused(): pl.pallas_call(functools.partial(fused_kernel, n_blk, n_aux, norm), out_s...]
where the time goes in v6:
time: 34.9 us; the launch traced here: 34.6 us
  Pallas kernels  33.4 us (96%)
  between operations  0.64 us (2%)
  local copies, waits for them, and re-layouts  0.61 us (2%)
    pallas_call x1, Pallas kernels, fused(): pl.pallas_call(functools.partial(fused_kernel, n_blk, n_aux, norm), out_s...  33.4 us

profile of v6, /device:TPU:0, one launch (start us, length us, event | category | flops | bytes accessed | tf_op | source)
XLA Modules:
  0.0 34.6 jit_solution(9366901110321347266)
XLA Ops:
  0.6 33.4 %fused.1 = f32[2,2,1024]{2,1,0:T(2,128)S(1)} custom-call(s32[8]{0:T(128)} %sizes_hbm.1, s32[4]{0:T(128)} %rows_hbm.1, s32[4]{0:T(128)} %bitcast.7, s32[4]{0:T(128)} %blocks_hbm.1, bf16[32,1024]{1,0:T(8,128)(2,1)} %adj_hbm.1, bf16[8,1024]{1,0:T(8,128)(2,1)} %occ_hbm.1, bf16[8,1024]{1,0:T(8,128)(2,1)} %vir_hbm.1, bf16[4,32,4,8,1024]{4,3,2,1,0:T(8,128)(2,1)} %bitcast.6), custom_call_target="tpu_custom_call" | custom-call | tf_op jit(solution)/shard_map/fused/pallas_call | solution.py:437
  34.0 0.6 %slice_bitcast_fusion = (f32[2,1024]{1,0:T(2,128)}, f32[2,1024]{1,0:T(2,128)}) fusion(f32[2,2,1024]{2,1,0:T(2,128)S(1)} %fused.1), kind=kLoop, calls=%fused_computation | loop fusion | bytes 32768 | tf_op jit(solution)/shard_map/squeeze | solution.py:682

commit v7 on v6

--- a/solution.py
+++ b/solution.py
@@ -395,27 +395,26 @@
     def done(ref, sem):
         pltpu.make_async_copy(ref, ref, sem).wait()
 
+    per_tile = 128 // BS
+    scales = [jnp.where(live(sizes[a * own + r]), norm, 0.0).astype(F32) for r in range(own)]
+
+    def write(which, sums):
+        lanes_all = iota(sums.shape, 1) // BS
+        parts = [jnp.where(lanes_all == g, sums, 0.0) for g in range(groups)]
+        both = exact(jnp.concatenate(parts, axis=0), fold(128, 128, minor, minor)).reshape(groups, own, SUB, 128)
+        lines = []
+        for m in range(pairs // 128):
+            first = m * per_tile
+            here = iota((SUB, 128), 0) == first % SUB + lanes_of
+            lines.append(jnp.sum(jnp.where(here, both[first // SUB], 0.0), axis=1))
+        flat = jnp.concatenate(lines, axis=1)
+        for r in range(own):
+            out_ref[which, r : r + 1, :] = flat[r : r + 1, :] * scales[r]
+
+    done(occ_got.at[pl.ds(0, n_aux - 1)], trade_sem.at[3])
+    write(0, jnp.sum(occ_got[...], axis=0))
     done(vir_got.at[pl.ds(0, n_dev - 1)], trade_sem.at[1])
-    vir_sum = jnp.sum(vir_got[...].astype(F32), axis=0)
-    done(occ_got.at[pl.ds(0, n_aux - 1)], trade_sem.at[3])
-    occ_sum = jnp.sum(occ_got[...], axis=0)
-
-    sums = jnp.concatenate([occ_sum, vir_sum], axis=0)
-    lanes_all = iota(sums.shape, 1) // BS
-    parts = [jnp.where(lanes_all == g, sums, 0.0) for g in range(groups)]
-    both = exact(jnp.concatenate(parts, axis=0), fold(128, 128, minor, minor))
-    both = both.reshape(groups, 2 * own, SUB, 128)
-    per_tile = 128 // BS
-    lines = []
-    for m in range(pairs // 128):
-        first = m * per_tile
-        here = iota((SUB, 128), 0) == first % SUB + lanes_of
-        lines.append(jnp.sum(jnp.where(here, both[first // SUB], 0.0), axis=1))
-    flat = jnp.concatenate(lines, axis=1)
-    for r in range(own):
-        scale = jnp.where(live(sizes[a * own + r]), norm, 0.0).astype(F32)
-        out_ref[0, r : r + 1, :] = flat[r : r + 1, :] * scale
-        out_ref[1, r : r + 1, :] = flat[own + r : own + r + 1, :] * scale
+    write(1, jnp.sum(vir_got[...].astype(F32), axis=0))
 
     done(vir_send.at[pl.ds(0, n_dev - 1)], trade_sem.at[0])
     done(occ_send.at[pl.ds(0, n_aux - 1)], trade_sem.at[2])

time: 34.9 us -> 34.9 us (level)
  no operation moved by 1% of the time
where the time goes in v7:
time: 34.9 us; the launch traced here: 34.6 us
  Pallas kernels  33.4 us (96%)
  between operations  0.64 us (2%)
  local copies, waits for them, and re-layouts  0.61 us (2%)
    pallas_call x1, Pallas kernels, fused(): pl.pallas_call(functools.partial(fused_kernel, n_blk, n_aux, norm), out_s...  33.4 us

profile of v7, /device:TPU:0, one launch (start us, length us, event | category | flops | bytes accessed | tf_op | source)
XLA Modules:
  0.0 34.6 jit_solution(8951295171027439391)
XLA Ops:
  0.6 33.4 %fused.1 = f32[2,2,1024]{2,1,0:T(2,128)S(1)} custom-call(s32[8]{0:T(128)} %sizes_hbm.1, s32[4]{0:T(128)} %rows_hbm.1, s32[4]{0:T(128)} %bitcast.7, s32[4]{0:T(128)} %blocks_hbm.1, bf16[32,1024]{1,0:T(8,128)(2,1)} %adj_hbm.1, bf16[8,1024]{1,0:T(8,128)(2,1)} %occ_hbm.1, bf16[8,1024]{1,0:T(8,128)(2,1)} %vir_hbm.1, bf16[4,32,4,8,1024]{4,3,2,1,0:T(8,128)(2,1)} %bitcast.6), custom_call_target="tpu_custom_call" | custom-call | tf_op jit(solution)/shard_map/fused/pallas_call | solution.py:436
  34.0 0.6 %slice_bitcast_fusion = (f32[2,1024]{1,0:T(2,128)}, f32[2,1024]{1,0:T(2,128)}) fusion(f32[2,2,1024]{2,1,0:T(2,128)S(1)} %fused.1), kind=kLoop, calls=%fused_computation | loop fusion | bytes 32768 | tf_op jit(solution)/shard_map/squeeze | solution.py:681
